TPU v7x, 256 devices: a whole 4x4x8 slice. The times are simulated.
256 devices in a mesh: var: 8 (over z), lon: 16 (over y_lo, x, core), lat: 2 (over y_hi).
Axes of the slice: x: 4, y: 4 (y_hi: 2, y_lo: 2; y = y_hi * 2 + y_lo), z: 8, core: 2. Of those that a mesh axis runs over, the one named last changes fastest.
Arguments:
- fields: bfloat16 [48, 2, 96, 192, 16], P(('var', 'lat'), None, None, 'lon'), may hold values from -6 to 6
- score_table: bfloat16 [48, 16, 8], replicated, may hold values from -120 to 120
- score_bias: float32 [48, 8], replicated, may hold values from -6 to 6
- value_table: bfloat16 [48, 16, 512], replicated, may hold values from -1.5 to 1.5
- value_bias: float32 [48, 512], replicated, may hold values from -6 to 6
- agg_weight: bfloat16 [512, 512], replicated, may hold values from -0.25 to 0.25
- qkv_weight: bfloat16 [2, 512, 1536], replicated, may hold values from -10 to 10
- proj_weight: bfloat16 [2, 512, 512], replicated, may hold values from -0.25 to 0.25
- up_weight: bfloat16 [512, 2048], replicated, may hold values from -0.25 to 0.25
- down_weight: bfloat16 [2048, 512], replicated, may hold values from -0.125 to 0.125
- norm_gains: float32 [4, 512], replicated, may hold values from 0.1 to 1.9
- decode_weight: bfloat16 [512, 768], replicated, may hold values from -0.25 to 0.25
- decode_bias: float32 [768], replicated, may hold values from -3 to 3
Outputs:
- forecast: bfloat16 [2, 96, 192, 768], P(None, ('var', 'lat'), 'lon')
All inputs are finite; a program needn't handle non-finite values.
Results may differ from a plain program's by a relative error of at most 0.025.
Values may be sent and summed in bfloat16 or wider, within the bound.
A program may use at most 128 MiB of HBM per device.

v0:
```python
import math

import jax
import jax.numpy as jnp
from jax import lax
from jax.sharding import PartitionSpec as P

WLEV = 2
WLAT = 6
WLON = 12


EPSILON = 1e-05


def copy_for_each(array, axis):
    copies = jnp.broadcast_to(array, (lax.axis_size(axis), *array.shape))
    return lax.all_to_all(copies, axis, split_axis=0, concat_axis=0, tiled=True)


def over_copies(array, axis):
    return copy_for_each(array, axis).max(axis=0)


def split_up(array, dim, size):
    before, after = (array.shape[:dim], array.shape[dim + 1 :])
    return jnp.moveaxis(array.reshape(*before, size, -1, *after), dim, 0)


def sum_at_owner(array, axis, dim):
    tiles = split_up(array, dim, lax.axis_size(axis))
    arrived = lax.all_to_all(tiles, axis, split_axis=0, concat_axis=0, tiled=True)
    return arrived.astype(jnp.float32).sum(axis=0)


def in_one_piece(arrays, axis, dim, along):
    ends, at = ([], 0)
    for a in arrays[:-1]:
        at += a.shape[along]
        ends.append(at)
    both = jnp.concatenate(arrays, axis=along)
    return tuple(jnp.split(sum_at_owner(both, axis, dim), ends, axis=along))


def padded(array, sides, width, wrap):
    for axis, dim in sides:
        size, length = (lax.axis_size(axis), array.shape[dim])
        up = [(i, (i + 1) % size) for i in range(size if wrap else size - 1)]
        down = [(j, i) for i, j in up]
        last = lax.slice_in_dim(array, length - width, length, axis=dim)
        leading = lax.slice_in_dim(array, 0, width, axis=dim)
        before = lax.ppermute(last, axis, up)
        after = lax.ppermute(leading, axis, down)
        array = jnp.concatenate([before, array, after], axis=dim)
    return array


def layer_norm(values, norm_gain):
    centre = jnp.mean(values, axis=-1, keepdims=True)
    shifted = values - centre
    spread = jnp.mean(shifted * shifted, axis=-1, keepdims=True)
    return shifted * lax.rsqrt(spread + EPSILON) * norm_gain


def var_scores(patches, score_tab, offsets):
    scores = jnp.einsum("vlrcp,vph->vlrch", patches, score_tab, preferred_element_type=jnp.float32)
    return scores + offsets[:, None, None, None, :]


def group_terms(patches, scores, top_score, table, offsets):
    levels, rows, cols, patch_size = patches.shape[1:]
    head_count = scores.shape[-1]
    width = table.shape[-1]

    def add_var(totals, pieces):
        patch, score, tab, offset = pieces
        weights = jnp.exp(score - top_score)
        values = (
            jnp.dot(patch.reshape(-1, patch_size), tab, preferred_element_type=jnp.float32) + offset
        )
        values = values.reshape(levels, rows, cols, head_count, width // head_count)
        return ((totals[0] + weights[..., None] * values, totals[1] + weights), None)

    start = (
        jnp.zeros((levels, rows, cols, head_count, width // head_count), jnp.float32),
        jnp.zeros((levels, rows, cols, head_count), jnp.float32),
    )
    sums, _ = lax.scan(add_var, start, (patches, scores, table, offsets))
    return sums


def attend(queries, keys_vals, allowed, head_count):
    windows, length, model_width = queries.shape
    head_dim = model_width // head_count
    query_heads = queries.reshape(windows, length, head_count, head_dim)
    key_heads = keys_vals[..., :model_width].reshape(windows, -1, head_count, head_dim)
    value_heads = keys_vals[..., model_width:].reshape(windows, -1, head_count, head_dim)
    scores = jnp.einsum(
        "bqhd,bkhd->bhqk", query_heads, key_heads, preferred_element_type=jnp.float32
    ) / math.sqrt(head_dim)
    if allowed is not None:
        scores = jnp.where(allowed[:, None], scores, -jnp.inf)
    scores = scores - jnp.max(scores, axis=-1, keepdims=True)
    raised = jnp.exp(scores)
    weights = (raised / jnp.sum(raised, axis=-1, keepdims=True)).astype(jnp.bfloat16)
    context = jnp.einsum(
        "bhqk,bkhd->bqhd", weights, value_heads, preferred_element_type=jnp.float32
    )
    return context.astype(jnp.bfloat16).reshape(windows, length, model_width)


def to_windows(source, window_sizes):
    level_size, row_size, col_size = window_sizes
    level_count, row_count, col_count, features = source.shape
    blocked = source.reshape(
        level_count // level_size,
        level_size,
        row_count // row_size,
        row_size,
        col_count // col_size,
        col_size,
        features,
    )
    blocked = blocked.transpose(0, 2, 4, 1, 3, 5, 6)
    return blocked.reshape(-1, level_size * row_size * col_size, features)


def from_windows(windowed, full_shape, window_sizes):
    level_size, row_size, col_size = window_sizes
    level_count, row_count, col_count, features = full_shape
    blocked = windowed.reshape(
        level_count // level_size,
        row_count // row_size,
        col_count // col_size,
        level_size,
        row_size,
        col_size,
        features,
    )
    return blocked.transpose(0, 3, 1, 4, 2, 5, 6).reshape(full_shape)


def per_device(
    fields,
    score_table,
    score_bias,
    value_table,
    value_bias,
    agg_weight,
    qkv_weight,
    proj_weight,
    up_weight,
    down_weight,
    norm_gains,
    decode_weight,
    decode_bias,
):
    groups = lax.axis_size(("var", "lat"))
    band_index = lax.axis_index(("var", "lat"))
    local_vars, levels, all_rows, band_cols, patch_size = fields.shape
    band_rows = all_rows // groups
    head_count = score_table.shape[2]
    model_width = agg_weight.shape[0]
    first_var = band_index * local_vars
    own_scores = lax.dynamic_slice_in_dim(score_table, first_var, local_vars, 0)
    own_offsets = lax.dynamic_slice_in_dim(score_bias, first_var, local_vars, 0)
    own_values = lax.dynamic_slice_in_dim(value_table, first_var, local_vars, 0)
    own_biases = lax.dynamic_slice_in_dim(value_bias, first_var, local_vars, 0)
    scores = var_scores(fields, own_scores, own_offsets)
    top_score = over_copies(jnp.max(scores, axis=0).astype(jnp.bfloat16), ("var", "lat")).astype(
        jnp.float32
    )
    numerator, denominator = group_terms(fields, scores, top_score, own_values, own_biases)
    numerator = numerator.reshape(levels, all_rows, band_cols, model_width)
    numerator, denominator = in_one_piece(
        (numerator.astype(jnp.bfloat16), denominator.astype(jnp.bfloat16)), ("var", "lat"), 1, 3
    )
    pooled = (
        numerator.reshape(levels, band_rows, band_cols, head_count, -1) / denominator[..., None]
    )
    pooled = pooled.reshape(levels, band_rows, band_cols, model_width).astype(jnp.bfloat16)
    latent = jnp.dot(pooled, agg_weight, preferred_element_type=jnp.float32)
    sizes = (WLEV, WLAT, WLON)
    normed = layer_norm(latent, norm_gains[0]).astype(jnp.bfloat16)
    projected = jnp.dot(normed, qkv_weight[0], preferred_element_type=jnp.float32).astype(
        jnp.bfloat16
    )
    windowed = to_windows(projected, sizes)
    context = attend(windowed[..., :model_width], windowed[..., model_width:], None, head_count)
    context = from_windows(context, (levels, band_rows, band_cols, model_width), sizes)
    hidden = latent + jnp.dot(context, proj_weight[0], preferred_element_type=jnp.float32)
    mixed = layer_norm(hidden, norm_gains[1]).astype(jnp.bfloat16)
    active = jax.nn.gelu(
        jnp.dot(mixed, up_weight, preferred_element_type=jnp.float32), approximate=True
    ).astype(jnp.bfloat16)
    latent = hidden + jnp.dot(active, down_weight, preferred_element_type=jnp.float32)
    level_half, row_half, col_half = (WLEV // 2, WLAT // 2, WLON // 2)
    normed = layer_norm(latent, norm_gains[2]).astype(jnp.bfloat16)
    query_weight = qkv_weight[1][:, :model_width]
    pair_weight = qkv_weight[1][:, model_width:]
    queries = jnp.dot(normed, query_weight, preferred_element_type=jnp.float32).astype(jnp.bfloat16)
    tall_frame = padded(normed, ((("var", "lat"), 1),), row_half, False)
    framed = padded(tall_frame, (("lon", 2),), col_half, True)
    framed = jnp.dot(framed, pair_weight, preferred_element_type=jnp.float32).astype(jnp.bfloat16)
    frame_rows = band_rows + 2 * row_half
    frame_cols = band_cols + 2 * col_half
    padded_queries = jnp.pad(queries, ((0, 0), (row_half, row_half), (col_half, col_half), (0, 0)))
    level_ids = (jnp.arange(levels) + level_half) // WLEV
    global_rows = band_index * band_rows + jnp.arange(frame_rows) - row_half
    valid_rows = ((global_rows >= 0) & (global_rows < groups * band_rows)).astype(jnp.int32)
    grid_shape = (levels, frame_rows, frame_cols, 1)
    level_grid = jnp.broadcast_to(level_ids[:, None, None, None], grid_shape)
    valid_grid = jnp.broadcast_to(valid_rows[None, :, None, None], grid_shape)
    level_windows = to_windows(jnp.roll(level_grid, -level_half, axis=0), sizes)[..., 0]
    valid_windows = to_windows(jnp.roll(valid_grid, -level_half, axis=0), sizes)[..., 0]
    allowed = (level_windows[:, :, None] == level_windows[:, None, :]) & (
        valid_windows[:, None, :] == 1
    )
    query_windows = to_windows(jnp.roll(padded_queries, -level_half, axis=0), sizes)
    pair_windows = to_windows(jnp.roll(framed, -level_half, axis=0), sizes)
    context = attend(query_windows, pair_windows, allowed, head_count)
    context = from_windows(context, (levels, frame_rows, frame_cols, model_width), sizes)
    context = jnp.roll(context, level_half, axis=0)[
        :, row_half : row_half + band_rows, col_half : col_half + band_cols
    ]
    latent = latent + jnp.dot(context, proj_weight[1], preferred_element_type=jnp.float32)
    final = layer_norm(latent, norm_gains[3]).astype(jnp.bfloat16)
    return (jnp.dot(final, decode_weight, preferred_element_type=jnp.float32) + decode_bias).astype(
        jnp.bfloat16
    )


def solution(mesh):
    return jax.shard_map(
        per_device,
        mesh=mesh,
        in_specs=(
            P(("var", "lat"), None, None, "lon", None),
            P(),
            P(),
            P(),
            P(),
            P(),
            P(),
            P(),
            P(),
            P(),
            P(),
            P(),
            P(),
        ),
        out_specs=P(None, ("var", "lat"), "lon", None),
        check_vma=False,
    )
```

profile of v0, /device:TPU:1, one launch (start us, length us, event | category | flops | bytes accessed | tf_op | source)
XLA Modules:
  0.0 301.4 jit_solution(12825338183627941072)
XLA Ops:
  4.2 11.7 %all-to-all-start = ((bf16[16,2,96,12,8]{2,4,3,1,0:T(8,128)(2,1)}), bf16[16,2,96,12,8]{2,4,3,1,0:T(8,128)(2,1)S(1)}, u32[]{:S(2)}, u32[]{:S(2)}) async-start(bf16[16,2,96,12,8]{2,4,3,1,0:T(8,128)(2,1)} %broadcast_in_dim.20), calls=%async_computation | async-start | bytes 1572864 | tf_op jit(solution)/shard_map/all_to_all | solution.py:18
  17.5 20.7 %all-to-all-done = bf16[16,2,96,12,8]{2,4,3,1,0:T(8,128)(2,1)S(1)} async-done(((bf16[16,2,96,12,8]{2,4,3,1,0:T(8,128)(2,1)}), bf16[16,2,96,12,8]{2,4,3,1,0:T(8,128)(2,1)S(1)}, u32[]{:S(2)}, u32[]{:S(2)}) %all-to-all-start) | async-done | bytes 589856 | tf_op jit(solution)/shard_map/all_to_all | solution.py:18
  40.0 91.4 %while.13 = (s32[]{:T(128)}, f32[2,96,12,8,64]{4,3,2,1,0:T(8,128)}, f32[2,96,12,8]{3,2,1,0:T(8,128)}, f32[3,2,96,12,8]{2,4,3,1,0:T(8,128)S(1)}, f32[2,96,12,8]{3...) while((s32[]{:T(128)}, f32[2,96,12,8,64]{4,3,2,1,0:T(8,128)}, ...), condition=%wide.region_3.4_spmd.clone, body=%wide.region_2.3_spmd.clone.sunk | while | flops 42522624 | bytes 29587584 | solution.py:88
  42.8 3.0 convolution_add_fusion.6
  45.7 8.0 %reshape.248 = f32[2,96,12,8,64]{4,3,2,1,0:T(8,128)} reshape(f32[2304,512]{1,0:T(8,128)} %convolution_add_fusion.6) | data formatting | bytes 9437184 | tf_op jit(solution)/shard_map/while/body/eval_jaxpr/reshape | solution.py:81
  55.5 3.5 %select_add_fusion.4 = (f32[2,96,12,8]{3,2,1,0:T(8,128)}, f32[2,96,12,8]{3,2,1,0:T(8,128)S(1)}) fusion(f32[2,96,12,8]{3,2,1,0:T(8,128)} %get-tuple-element.235, pred[]{:T(512)S(6)} %compare.15, f32[2,96,12,8]{3,2,1,0:T(8,128)} %get-tuple-element.247, f32[1,2,96,12,8]{4,3,2,1,0:T(8,128)} %copy.154), kind=kLoop, calls=%fused_computation.4.clone.1 | loop fusion | flops 55296 | bytes 368641 | tf_op jit(solution)/shard_map/while/body/eval_jaxpr/add | solution.py:82
  58.9 9.9 %select_add_fusion.5 = f32[2,96,12,8,64]{4,3,2,1,0:T(8,128)} fusion(f32[2,96,12,8,64]{4,3,2,1,0:T(8,128)} %get-tuple-element.234, f32[2,96,12,8,64]{4,3,2,1,0:T(8,128)} %reshape.248, f32[2,96,12,8]{3,2,1,0:T(8,128)S(1)} %get-tuple-element.221, pred[]{:T(512)S(6)} %compare.15), kind=kLoop, calls=%fused_computation.clone.1 | loop fusion | flops 3538944 | bytes 14229505 | tf_op jit(solution)/shard_map/while/body/eval_jaxpr/add | solution.py:82
  71.5 3.0 convolution_add_fusion.6
  74.5 8.0 %reshape.248 = f32[2,96,12,8,64]{4,3,2,1,0:T(8,128)} reshape(f32[2304,512]{1,0:T(8,128)} %convolution_add_fusion.6) | data formatting | bytes 9437184 | tf_op jit(solution)/shard_map/while/body/eval_jaxpr/reshape | solution.py:81
  84.2 4.0 %select_add_fusion.4 = (f32[2,96,12,8]{3,2,1,0:T(8,128)}, f32[2,96,12,8]{3,2,1,0:T(8,128)S(1)}) fusion(f32[2,96,12,8]{3,2,1,0:T(8,128)} %get-tuple-element.235, pred[]{:T(512)S(6)} %compare.15, f32[2,96,12,8]{3,2,1,0:T(8,128)} %get-tuple-element.247, f32[1,2,96,12,8]{4,3,2,1,0:T(8,128)} %copy.154), kind=kLoop, calls=%fused_computation.4.clone.1 | loop fusion | flops 55296 | bytes 368641 | tf_op jit(solution)/shard_map/while/body/eval_jaxpr/add | solution.py:82
  88.2 11.9 %select_add_fusion.5 = f32[2,96,12,8,64]{4,3,2,1,0:T(8,128)} fusion(f32[2,96,12,8,64]{4,3,2,1,0:T(8,128)} %get-tuple-element.234, f32[2,96,12,8,64]{4,3,2,1,0:T(8,128)} %reshape.248, f32[2,96,12,8]{3,2,1,0:T(8,128)S(1)} %get-tuple-element.221, pred[]{:T(512)S(6)} %compare.15), kind=kLoop, calls=%fused_computation.clone.1 | loop fusion | flops 3538944 | bytes 14229505 | tf_op jit(solution)/shard_map/while/body/eval_jaxpr/add | solution.py:82
  102.8 3.0 convolution_add_fusion.6
  105.8 8.0 %reshape.248 = f32[2,96,12,8,64]{4,3,2,1,0:T(8,128)} reshape(f32[2304,512]{1,0:T(8,128)} %convolution_add_fusion.6) | data formatting | bytes 9437184 | tf_op jit(solution)/shard_map/while/body/eval_jaxpr/reshape | solution.py:81
  115.5 4.0 %select_add_fusion.4 = (f32[2,96,12,8]{3,2,1,0:T(8,128)}, f32[2,96,12,8]{3,2,1,0:T(8,128)S(1)}) fusion(f32[2,96,12,8]{3,2,1,0:T(8,128)} %get-tuple-element.235, pred[]{:T(512)S(6)} %compare.15, f32[2,96,12,8]{3,2,1,0:T(8,128)} %get-tuple-element.247, f32[1,2,96,12,8]{4,3,2,1,0:T(8,128)} %copy.154), kind=kLoop, calls=%fused_computation.4.clone.1 | loop fusion | flops 55296 | bytes 368641 | tf_op jit(solution)/shard_map/while/body/eval_jaxpr/add | solution.py:82
  119.5 11.9 %select_add_fusion.5 = f32[2,96,12,8,64]{4,3,2,1,0:T(8,128)} fusion(f32[2,96,12,8,64]{4,3,2,1,0:T(8,128)} %get-tuple-element.234, f32[2,96,12,8,64]{4,3,2,1,0:T(8,128)} %reshape.248, f32[2,96,12,8]{3,2,1,0:T(8,128)S(1)} %get-tuple-element.221, pred[]{:T(512)S(6)} %compare.15), kind=kLoop, calls=%fused_computation.clone.1 | loop fusion | flops 3538944 | bytes 14229505 | tf_op jit(solution)/shard_map/while/body/eval_jaxpr/add | solution.py:82
  131.4 6.8 %convert_element_type.81 = bf16[2,96,12,8,64]{4,3,2,1,0:T(8,128)(2,1)} convert(f32[2,96,12,8,64]{4,3,2,1,0:T(8,128)} %get-tuple-element.48) | non-fusion elementwise | flops 1179648 | bytes 7077888 | tf_op jit(solution)/shard_map/convert_element_type | solution.py:176
  138.2 7.8 %copy.108 = bf16[2,96,12,8,64]{1,4,3,2,0:T(8,128)(2,1)} copy(bf16[2,96,12,8,64]{4,3,2,1,0:T(8,128)(2,1)} %convert_element_type.81) | data formatting | bytes 4718592 | tf_op jit(solution)/shard_map/convert_element_type | solution.py:176
  147.9 4.2 %pad_maximum_fusion = bf16[2,96,12,520]{1,3,2,0:T(8,128)(2,1)} fusion(bf16[2,96,12,8]{1,3,2,0:T(8,128)(2,1)S(1)} %copy.109, bf16[2,96,12,512]{1,3,2,0:T(8,128)(2,1)} %bitcast.155), kind=kLoop, calls=%fused_computation.18 | loop fusion | flops 4792320 | bytes 4792320 | tf_op jit(solution)/shard_map/concatenate | solution.py:41
  152.0 7.6 %copy.110 = bf16[2,96,12,520]{3,0,2,1:T(2,128)(2,1)} copy(bf16[2,96,12,520]{1,3,2,0:T(8,128)(2,1)} %pad_maximum_fusion) | data formatting | bytes 4792320 | tf_op jit(solution)/shard_map/concatenate | solution.py:41
  159.6 5.4 %all-to-all-start.1 = ((bf16[16,2,6,12,520]{4,1,3,2,0:T(2,128)(2,1)}), bf16[16,2,6,12,520]{4,1,3,2,0:T(2,128)(2,1)}, u32[]{:S(2)}, u32[]{:S(2)}) async-start(bf16[16,2,6,12,520]{4,1,3,2,0:T(2,128)(2,1)} %bitcast.156), calls=%async_computation.1 | async-start | bytes 5898240 | tf_op jit(solution)/shard_map/all_to_all | solution.py:32
  168.1 2.7 slice_bitcast_fusion
  170.8 63.0 %all-to-all-done.1 = bf16[16,2,6,12,520]{4,1,3,2,0:T(2,128)(2,1)} async-done(((bf16[16,2,6,12,520]{4,1,3,2,0:T(2,128)(2,1)}), bf16[16,2,6,12,520]{4,1,3,2,0:T(2,128)(2,1)}, u32[]{:S(2)}, u32[]{:S(2)}) %all-to-all-start.1) | async-done | bytes 2396192 | tf_op jit(solution)/shard_map/all_to_all | solution.py:32
  233.8 4.6 %convert_reduce_fusion = f32[2,6,12,520]{3,0,2,1:T(2,128)S(1)} fusion(bf16[16,2,6,12,520]{4,1,3,2,0:T(2,128)(2,1)} %all-to-all-done.1), kind=kLoop, calls=%fused_computation.13 | loop fusion | flops 2321280 | bytes 2695680 | tf_op jit(solution)/shard_map/reduce_sum | solution.py:33
  249.0 3.0 %fusion.102 = (f32[2,6,12]{2,1,0:T(8,128)S(1)}, f32[2,6,12,512]{3,2,1,0:T(8,128)S(1)}) fusion(f32[2,6,12,512]{3,2,1,0:T(8,128)S(1)} %get-tuple-element.163, bf16[2048,512]{1,0:T(8,128)(2,1)S(1)} %copy-done, bf16[512,2048]{1,0:T(8,128)(2,1)} %param.23, f32[512]{0:T(512)S(1)} %bitcast.169, f32[2,6,12]{2,1,0:T(8,128)S(1)} %add_rsqrt_fusion.2, ...), kind=kOutput, calls=%fused_computation.150 | convolution fusion | flops 607076224 | bytes 4787904 | tf_op jit(solution)/shard_map/dot_general | solution.py:196
  252.4 2.2 collective-permute-start
  257.3 4.2 %collective-permute-done.1 = bf16[2,3,12,512]{3,2,1,0:T(8,128)(2,1)S(1)} collective-permute-done((bf16[2,3,12,512]{3,2,1,0:T(8,128)(2,1)S(1)}, bf16[2,3,12,512]{3,2,1,0:T(8,128)(2,1)S(1)}, u32[]{:S(2)}, u32[]{:S(2)}) %collective-permute-start.1) | collective-permute-done | bytes 73760 | tf_op jit(solution)/shard_map/ppermute | solution.py:53
  261.7 4.8 %collective-permute-start.2 = (bf16[2,12,6,512]{3,2,1,0:T(8,128)(2,1)S(1)}, bf16[2,12,6,512]{3,2,1,0:T(8,128)(2,1)}, u32[]{:S(2)}, u32[]{:S(2)}) collective-permute-start(bf16[2,12,6,512]{3,2,1,0:T(8,128)(2,1)S(1)} %get-tuple-element.144), channel_id=1, source_target_pairs={{0,2},{2,4},{4,6},{6,8},{8,10},{10,12},{12,14},{14,16},{16,18},{18... | collective-permute-start | bytes 442376 | tf_op jit(solution)/shard_map/ppermute | solution.py:52
  269.4 2.5 collective-permute-done.3
  275.6 2.3 copy.118
  277.9 3.2 %reshape.229 = bf16[4,144,1024]{2,0,1:T(4,128)(2,1)S(1)} reshape(bf16[1,2,2,2,6,12,1024]{6,2,1,5,4,3,0:T(2,128)(2,1)} %copy.118) | data formatting | bytes 2359296 | tf_op jit(solution)/shard_map/reshape | solution.py:125
  282.4 2.3 copy.123
  284.8 2.2 copy.119
  (124 shorter events, 61.5 us)
Async XLA Ops:
  0.0 249.0 %copy-start = (bf16[2048,512]{1,0:T(8,128)(2,1)S(1)}, bf16[2048,512]{1,0:T(8,128)(2,1)}, u32[]{:S(2)}) copy-start(bf16[2048,512]{1,0:T(8,128)(2,1)} %param.24) | copy-start | bytes 6291460
  4.2 34.1 %all-to-all-start = ((bf16[16,2,96,12,8]{2,4,3,1,0:T(8,128)(2,1)}), bf16[16,2,96,12,8]{2,4,3,1,0:T(8,128)(2,1)S(1)}, u32[]{:S(2)}, u32[]{:S(2)}) async-start(bf16[16,2,96,12,8]{2,4,3,1,0:T(8,128)(2,1)} %broadcast_in_dim.20), calls=%async_computation | async-start | bytes 1572864 | tf_op jit(solution)/shard_map/all_to_all | solution.py:18
  159.6 7.6 %copy-start.8 = (f32[4,512]{1,0:T(4,128)S(1)}, f32[4,512]{1,0:T(4,128)}, u32[]{:S(2)}) copy-start(f32[4,512]{1,0:T(4,128)} %param.25) | copy-start | bytes 24580
  159.6 74.2 %all-to-all-start.1 = ((bf16[16,2,6,12,520]{4,1,3,2,0:T(2,128)(2,1)}), bf16[16,2,6,12,520]{4,1,3,2,0:T(2,128)(2,1)}, u32[]{:S(2)}, u32[]{:S(2)}) async-start(bf16[16,2,6,12,520]{4,1,3,2,0:T(2,128)(2,1)} %bitcast.156), calls=%async_computation.1 | async-start | bytes 5898240 | tf_op jit(solution)/shard_map/all_to_all | solution.py:32
  243.9 1.6 copy-start.6
  252.1 9.5 %copy-start.2 = (f32[2,6,12,512]{3,2,1,0:T(8,128)}, f32[2,6,12,512]{3,2,1,0:T(8,128)S(1)}, u32[]{:S(2)}) copy-start(f32[2,6,12,512]{3,2,1,0:T(8,128)S(1)} %get-tuple-element.165) | copy-start | bytes 884740
  252.4 4.8 %collective-permute-start = (bf16[2,3,12,512]{3,2,1,0:T(8,128)(2,1)S(1)}, bf16[2,3,12,512]{3,2,1,0:T(8,128)(2,1)S(1)}, u32[]{:S(2)}, u32[]{:S(2)}) collective-permute-start(bf16[2,3,12,512]{3,2,1,0:T(8,128)(2,1)S(1)} %get-tuple-element.148), channel_id=1, source_target_pairs={{0,1},{1,32},{32,33},{33,64},{64,65},{65,96},{96,97},{97,128},{128... | collective-permute-start | bytes 221192 | tf_op jit(solution)/shard_map/ppermute | solution.py:52
  254.7 6.9 %collective-permute-start.1 = (bf16[2,3,12,512]{3,2,1,0:T(8,128)(2,1)S(1)}, bf16[2,3,12,512]{3,2,1,0:T(8,128)(2,1)S(1)}, u32[]{:S(2)}, u32[]{:S(2)}) collective-permute-start(bf16[2,3,12,512]{3,2,1,0:T(8,128)(2,1)S(1)} %get-tuple-element.149), channel_id=1, source_target_pairs={{1,0},{32,1},{33,32},{64,33},{65,64},{96,65},{97,96},{128,97},{129... | collective-permute-start | bytes 221192 | tf_op jit(solution)/shard_map/ppermute | solution.py:53
  261.7 7.7 %collective-permute-start.2 = (bf16[2,12,6,512]{3,2,1,0:T(8,128)(2,1)S(1)}, bf16[2,12,6,512]{3,2,1,0:T(8,128)(2,1)}, u32[]{:S(2)}, u32[]{:S(2)}) collective-permute-start(bf16[2,12,6,512]{3,2,1,0:T(8,128)(2,1)S(1)} %get-tuple-element.144), channel_id=1, source_target_pairs={{0,2},{2,4},{4,6},{6,8},{8,10},{10,12},{12,14},{14,16},{16,18},{18... | collective-permute-start | bytes 442376 | tf_op jit(solution)/shard_map/ppermute | solution.py:52
  266.4 5.5 %collective-permute-start.3 = (bf16[2,12,6,512]{3,2,1,0:T(8,128)(2,1)S(1)}, bf16[2,12,6,512]{3,2,1,0:T(8,128)(2,1)}, u32[]{:S(2)}, u32[]{:S(2)}) collective-permute-start(bf16[2,12,6,512]{3,2,1,0:T(8,128)(2,1)S(1)} %get-tuple-element.145), channel_id=1, source_target_pairs={{2,0},{4,2},{6,4},{8,6},{10,8},{12,10},{14,12},{16,14},{18,16},{20... | collective-permute-start | bytes 442376 | tf_op jit(solution)/shard_map/ppermute | solution.py:53
  282.4 4.6 %copy-start.1 = (bf16[4,144,8,64]{3,2,0,1:T(8,128)(2,1)S(1)}, bf16[4,144,8,64]{3,2,0,1:T(8,128)(2,1)}, u32[]{:S(2)}) copy-start(bf16[4,144,8,64]{3,2,0,1:T(8,128)(2,1)} %reshape_reshape.6) | copy-start | bytes 1769476
  287.0 2.1 copy-start.7
  289.1 1.7 copy-start.4
  297.4 1.0 copy-start.3
  297.6 2.4 copy-start.9
  298.4 1.7 copy-start.5
where the time goes:
time: 305 us; the launch traced here: 301 us
  waiting for transfers between devices  90.5 us (30%)
  local copies, waits for them, and re-layouts  90.4 us (30%)
  other arithmetic  64.6 us (21%)
  matrix products  29.8 us (10%)
  starting transfers between devices  25.5 us (8%)
    all_to_all x1, waiting for transfers between devices, sum_at_owner(): lax.all_to_all(tiles, axis, split_axis=0, concat_axis=0, tiled=True)  63 us
    add x3, other arithmetic, add_var(): totals[0] + weights[..., None] * values  33.7 us
    reshape x3, local copies, waits for them, and re-layouts, add_var(): values = values.reshape(levels, rows, cols, head_count, width // head_count)  23.9 us
    all_to_all x1, waiting for transfers between devices, copy_for_each(): return lax.all_to_all(copies, axis, split_axis=0, concat_axis=0, tiled=True)  20.7 us
    all_to_all x1, starting transfers between devices, copy_for_each(): return lax.all_to_all(copies, axis, split_axis=0, concat_axis=0, tiled=True)  11.7 us
    add x3, other arithmetic, add_var(): totals[1] + weights  11.4 us
    dynamic_slice x15, local copies, waits for them, and re-layouts, group_terms(): sums, _ = lax.scan(add_var, start, (patches, scores, table, offsets))  9.25 us
    dot_general x3, matrix products, add_var(): jnp.dot(patch.reshape(-1, patch_size), tab, preferred_element_type=jnp.fl...  8.88 us
  transfers between devices with their start and end apart: 6, of which 4 were waited for; matrix products, arithmetic and copies ran while one was open for 4% of the time, Pallas kernels for 0%

commit v1 on v0

v1 whole, which is shorter than its diff:
```python
import functools

import jax
import jax.numpy as jnp
import numpy as np
from jax import lax
from jax.experimental import pallas as pl
from jax.experimental.pallas import tpu as pltpu
from jax.sharding import PartitionSpec as P

MESH = pl.DeviceIdType.MESH
EPSILON = 1e-05
F32 = jnp.float32
BF16 = jnp.bfloat16

GROUPS = 16
LONS = 16
LEV, ROWS, COLS = 2, 6, 12
CELLS = LEV * ROWS * COLS
LOCAL_VARS, PATCH, HEADS, HEAD_DIM = 3, 16, 8, 64
VARS = GROUPS * LOCAL_VARS
D, FF = 512, 2048
SLOT = 64
KDIM = GROUPS * SLOT
QUAD = 48
QUAD_CELLS = 36
SENT = 40


def cell_index(row, col, lev):
    return (row * COLS + col) * LEV + lev


def band_selector():
    out = np.zeros((GROUPS * 8, GROUPS * ROWS), np.float32)
    for band in range(GROUPS):
        for row in range(ROWS):
            out[band * 8 + row, band * ROWS + row] = 1
    return out


def cell_selector():
    out = np.zeros((CELLS, LEV * COLS * 8), np.float32)
    for lev in range(LEV):
        for col in range(COLS):
            for row in range(ROWS):
                out[cell_index(row, col, lev), (lev * COLS + col) * 8 + row] = 1
    return out


def quad_selector():
    out = np.zeros((4 * QUAD, CELLS), np.float32)
    for row in range(ROWS):
        for col in range(COLS):
            for lev in range(LEV):
                quad = (row // 3) * 2 + col // 6
                place = ((row % 3) * 6 + col % 6) * LEV + lev
                out[quad * QUAD + place, cell_index(row, col, lev)] = 1
    return out


def weight_spread():
    out = np.zeros((128, KDIM), np.float32)
    for group in range(GROUPS):
        for var in range(LOCAL_VARS):
            v, at = group * LOCAL_VARS + var, group * SLOT
            out[v, at + var * PATCH : at + (var + 1) * PATCH] = 1
            out[v, at + 48 + var] = 1
            out[v, at + 51 + var] = 1
    return out


def bias_rows():
    high = np.zeros((GROUPS * 8, VARS), np.float32)
    low = np.zeros((GROUPS * 8, VARS), np.float32)
    for group in range(GROUPS):
        for var in range(LOCAL_VARS):
            high[group * 8 + var, group * LOCAL_VARS + var] = 1
            low[group * 8 + 3 + var, group * LOCAL_VARS + var] = 1
    return high, low


def dot(a, b):
    return jnp.dot(a, b, preferred_element_type=F32)


def dot_t(a, b):
    return lax.dot_general(a, b, (((1,), (1,)), ((), ())), preferred_element_type=F32)


def layer_norm(values, gain):
    shifted = values - jnp.mean(values, axis=-1, keepdims=True)
    spread = jnp.mean(shifted * shifted, axis=-1, keepdims=True)
    return shifted * lax.rsqrt(spread + EPSILON) * gain


def lane_low(rows):
    return lax.broadcasted_iota(jnp.int32, (rows, 128), 1) < HEAD_DIM


def attention_pair(q, k, v, allowed):
    q_low, k_low = lane_low(q.shape[0]), lane_low(k.shape[0])
    total = None
    for low in (True, False):
        q_own = jnp.where(q_low == low, q, jnp.zeros_like(q))
        v_own = jnp.where(k_low == low, v, jnp.zeros_like(v))
        scores = dot_t(q_own, k) * (1.0 / 8.0)
        if allowed is not None:
            scores = jnp.where(allowed, scores, -jnp.inf)
        raised = jnp.exp(scores - jnp.max(scores, axis=-1, keepdims=True))
        probs = (raised * (1.0 / jnp.sum(raised, axis=-1, keepdims=True))).astype(BF16)
        part = dot(probs, v_own)
        total = part if total is None else total + part
    return total.astype(BF16)


def body(
    fields_ref,
    band_sel_ref,
    score_tab_ref,
    score_bias_ref,
    value_bias_ref,
    gains_ref,
    decode_bias_ref,
    high_ref,
    low_ref,
    ones_ref,
    cell_sel_hbm,
    quad_sel_hbm,
    quad_back_hbm,
    spread_hbm,
    value_tab_hbm,
    agg_hbm,
    qkv_hbm,
    proj_hbm,
    up_hbm,
    down_hbm,
    decode_hbm,
    out_ref,
    outgoing,
    incoming,
    cell_sel,
    quad_sel,
    quad_back,
    spread,
    table,
    agg,
    qkv_w,
    proj_w,
    up_w,
    down_w,
    decode_w,
    score_w,
    pool_in,
    pooled,
    normed_q,
    kv2,
    context,
    send_sem,
    recv_sem,
    halo_send,
    halo_recv,
    load_sem,
):
    var, lon, lat = lax.axis_index("var"), lax.axis_index("lon"), lax.axis_index("lat")
    band = var * 2 + lat
    up_band, down_band = lax.rem(band + GROUPS - 1, GROUPS), lax.rem(band + 1, GROUPS)
    left, right = lax.rem(lon + LONS - 1, LONS), lax.rem(lon + 1, LONS)

    def device(of_band, of_lon):
        return (of_band // 2, of_lon, lax.rem(of_band, 2))

    barrier = pltpu.get_barrier_semaphore()
    peers = [device(lax.rem(band + k, GROUPS), lon) for k in range(1, GROUPS)]
    peers += [device(b, c) for b in (band, up_band, down_band) for c in (left, right)]
    for peer in peers:
        pl.semaphore_signal(barrier, inc=1, device_id=peer, device_id_type=MESH)

    loads = [
        (value_tab_hbm, table.at[:, 0:48, :]),
        (cell_sel_hbm, cell_sel),
        (spread_hbm, spread),
        (agg_hbm, agg),
        (qkv_hbm.at[0], qkv_w.at[0]),
        (proj_hbm, proj_w),
        (up_hbm, up_w),
        (down_hbm, down_w),
        (quad_sel_hbm, quad_sel),
        (qkv_hbm.at[1], qkv_w.at[1]),
        (quad_back_hbm, quad_back),
        (decode_hbm, decode_w),
    ]
    loads = [pltpu.make_async_copy(a, b, load_sem.at[i]) for i, (a, b) in enumerate(loads)]
    for load in loads:
        load.start()
    (
        got_table,
        got_cells,
        got_spread,
        got_agg,
        got_qkv0,
        got_proj,
        got_up,
        got_down,
        got_quad,
        got_qkv1,
        got_back,
        got_decode,
    ) = loads

    band_sel = band_sel_ref[...]
    gap = jnp.zeros((16, GROUPS * ROWS), BF16)
    for col in range(COLS):
        parts = []
        for lev in range(LEV):
            parts += [fields_ref[v, lev, col] for v in range(LOCAL_VARS)] + [gap]
        turned = dot_t(band_sel, jnp.concatenate(parts, axis=0))
        outgoing[:, col] = turned.reshape(GROUPS, 8, 128).astype(BF16)

    pl.semaphore_wait(barrier, len(peers))

    sends = []
    for k in range(1, GROUPS):
        to = lax.rem(band + k, GROUPS)
        copy = pltpu.make_async_remote_copy(
            src_ref=outgoing.at[to],
            dst_ref=incoming.at[band],
            send_sem=send_sem.at[k],
            recv_sem=recv_sem.at[band],
            device_id=device(to, lon),
            device_id_type=MESH,
        )
        copy.start()
        sends.append(copy)
    own = pltpu.make_async_copy(outgoing.at[band], incoming.at[band], send_sem.at[0])
    own.start()

    row_var = (
        3 * lax.broadcasted_iota(jnp.int32, (GROUPS, 4, PATCH, 128), 0)
        + lax.broadcasted_iota(jnp.int32, (GROUPS, 4, PATCH, 128), 1)
    )
    part = lax.broadcasted_iota(jnp.int32, (GROUPS, 4, PATCH, 128), 1)
    lane = lax.broadcasted_iota(jnp.int32, (GROUPS, 4, PATCH, 128), 3)
    match = (row_var == lane) & (part < 3)
    for h in range(HEADS):
        tab = jnp.broadcast_to(
            score_tab_ref[h].astype(F32)[None, None], (GROUPS, 4, PATCH, 128)
        )
        score_w[:, h * 128 : (h + 1) * 128] = (
            jnp.where(match, tab, 0.0).reshape(KDIM, 128).astype(BF16)
        )
    bias = value_bias_ref[...]
    bias_high = bias.astype(BF16)
    bias_low = (bias - bias_high.astype(F32)).astype(BF16)
    rows = dot(high_ref[...], bias_high) + dot(low_ref[...], bias_low)
    table[:, 48:56, :] = rows.reshape(GROUPS, 8, D).astype(BF16)
    table[:, 56:64, :] = jnp.zeros((GROUPS, 8, D), BF16)
    normed_q[:, SENT:QUAD, :] = jnp.zeros((16, QUAD - SENT, D), BF16)

    own.wait()
    for k in range(1, GROUPS):
        source = lax.rem(band + GROUPS - k, GROUPS)
        pltpu.make_async_remote_copy(
            src_ref=outgoing.at[source],
            dst_ref=incoming.at[source],
            send_sem=send_sem.at[k],
            recv_sem=recv_sem.at[source],
            device_id=device(source, lon),
            device_id_type=MESH,
        ).wait_recv()

    got_cells.wait()
    half = COLS * 8
    low_half = lane_low(half)
    for j in range(GROUPS // 2):
        first = incoming[2 * j].astype(F32).reshape(half, 128)
        second = incoming[2 * j + 1].astype(F32).reshape(half, 128)
        at = slice(j * 128, (j + 1) * 128)
        pool_in[0:half, at] = jnp.where(low_half, first, pltpu.roll(second, 64, 1)).astype(BF16)
        pool_in[half : 2 * half, at] = jnp.where(low_half, pltpu.roll(first, 64, 1), second).astype(BF16)
    cells = (dot(cell_sel[...], pool_in[...]) + ones_ref[...]).astype(BF16)

    got_spread.wait()
    got_table.wait()
    lane128 = lax.broadcasted_iota(jnp.int32, (CELLS, 128), 1)
    real = lane128 < VARS
    low_cells = lane_low(CELLS)
    all_table = table[...].reshape(KDIM, D)
    for pair in range(HEADS // 2):
        kept = None
        for side in range(2):
            h = 2 * pair + side
            at = slice(h * 128, (h + 1) * 128)
            scores = dot(cells, score_w[:, at]) + score_bias_ref[h : h + 1, :]
            scores = jnp.where(real, scores, -jnp.inf)
            top = jnp.max(scores, axis=-1, keepdims=True)
            weights = jnp.exp(scores - top).astype(BF16)
            total = jnp.sum(weights.astype(F32), axis=-1, keepdims=True)
            spread_w = dot(weights, spread[...]).astype(BF16)
            sums = dot(cells * spread_w, all_table[:, pair * 128 : (pair + 1) * 128])
            mean = sums * (1.0 / total)
            kept = mean if kept is None else jnp.where(low_cells, kept, mean)
        pooled[:, pair * 128 : (pair + 1) * 128] = kept.astype(BF16)

    got_agg.wait()
    latent = dot(pooled[...], agg[...])

    normed = layer_norm(latent, gains_ref[0:1, :]).astype(BF16)
    got_qkv0.wait()
    qkv = dot(normed, qkv_w[0]).astype(BF16)
    for pair in range(HEADS // 2):
        at = pair * 128
        context[0:CELLS, at : at + 128] = attention_pair(
            qkv[:, at : at + 128],
            qkv[:, D + at : D + at + 128],
            qkv[:, 2 * D + at : 2 * D + at + 128],
            None,
        )
    got_proj.wait()
    hidden = latent + dot(context[0:CELLS, :], proj_w[0])

    mixed = layer_norm(hidden, gains_ref[1:2, :]).astype(BF16)
    got_up.wait()
    got_down.wait()
    latent = hidden
    for j in range(FF // D):
        at = slice(j * D, (j + 1) * D)
        active = jax.nn.gelu(dot(mixed, up_w[:, at]), approximate=True).astype(BF16)
        latent = latent + dot(active, down_w[at, :])

    normed = layer_norm(latent, gains_ref[2:3, :]).astype(BF16)
    got_quad.wait()
    quads = dot(quad_sel[...], normed).astype(BF16)
    halo = []
    for quad in range(4):
        normed_q[4 * quad] = quads[quad * QUAD : (quad + 1) * QUAD]
        row_half, col_half = quad // 2, quad % 2
        to_band = up_band if row_half == 0 else down_band
        to_lon = left if col_half == 0 else right
        targets = [
            (device(to_band, to_lon), (1 - row_half) * 2 + 1 - col_half, 3),
            (device(to_band, lon), (1 - row_half) * 2 + col_half, 2),
            (device(band, to_lon), row_half * 2 + 1 - col_half, 1),
        ]
        for target, window, slot in targets:
            copy = pltpu.make_async_remote_copy(
                src_ref=normed_q.at[4 * quad, 0:SENT],
                dst_ref=normed_q.at[4 * window + slot, 0:SENT],
                send_sem=halo_send.at[3 * quad + slot - 1],
                recv_sem=halo_recv.at[3 * window + slot - 1],
                device_id=target,
                device_id_type=MESH,
            )
            copy.start()
            halo.append(copy)

    got_qkv1.wait()
    queries = dot(quads, qkv_w[1, :, 0:D]).astype(BF16)
    row_lev = lax.broadcasted_iota(jnp.int32, (QUAD, 4 * QUAD), 0) % 2
    key = lax.broadcasted_iota(jnp.int32, (QUAD, 4 * QUAD), 1)
    place = key % QUAD
    same = (row_lev == place % 2) & (place < QUAD_CELLS)
    near = key < 2 * QUAD
    got_back.wait()

    for copy in halo:
        copy.wait_recv()
    kv2[...] = dot(normed_q[...].reshape(16 * QUAD, D), qkv_w[1, :, D : 3 * D]).astype(BF16)
    for quad in range(4):
        edge = band == (0 if quad // 2 == 0 else GROUPS - 1)
        allowed = same & (near | jnp.logical_not(edge))
        mine = slice(quad * QUAD, (quad + 1) * QUAD)
        keys = slice(quad * 4 * QUAD, (quad + 1) * 4 * QUAD)
        for pair in range(HEADS // 2):
            at = pair * 128
            context[mine, at : at + 128] = attention_pair(
                queries[mine, at : at + 128],
                kv2[keys, at : at + 128],
                kv2[keys, D + at : D + at + 128],
                allowed,
            )
    back = dot(quad_back[...], context[...]).astype(BF16)
    latent = latent + dot(back, proj_w[1])
    final = layer_norm(latent, gains_ref[3:4, :]).astype(BF16)
    got_decode.wait()
    out_ref[...] = (dot(final, decode_w[...]) + decode_bias_ref[...]).astype(BF16)

    for copy in sends:
        copy.wait_send()
    for copy in halo:
        copy.wait_send()


def per_device(
    fields,
    score_table,
    score_bias,
    value_table,
    value_bias,
    agg_weight,
    qkv_weight,
    proj_weight,
    up_weight,
    down_weight,
    norm_gains,
    decode_weight,
    decode_bias,
):
    high, low = bias_rows()
    quads = quad_selector()
    ones = np.zeros((1, KDIM), np.float32)
    for group in range(GROUPS):
        ones[0, group * SLOT + 48 : group * SLOT + 54] = 1
    scores = jnp.pad(score_table.transpose(2, 1, 0), ((0, 0), (0, 0), (0, 128 - VARS)))
    offsets = jnp.pad(score_bias.T, ((0, 0), (0, 128 - VARS)))
    near = [
        fields.transpose(0, 1, 3, 4, 2),
        jnp.asarray(band_selector(), BF16),
        scores,
        offsets,
        value_bias,
        norm_gains,
        decode_bias.reshape(1, -1),
        jnp.asarray(high, BF16),
        jnp.asarray(low, BF16),
        jnp.asarray(ones, F32),
    ]
    far = [
        jnp.asarray(cell_selector(), BF16),
        jnp.asarray(quads, BF16),
        jnp.asarray(quads.T, BF16),
        jnp.asarray(weight_spread(), BF16),
        value_table.reshape(GROUPS, LOCAL_VARS * PATCH, D),
        agg_weight,
        qkv_weight,
        proj_weight,
        up_weight,
        down_weight,
        decode_weight,
    ]
    vmem = pl.BlockSpec(memory_space=pltpu.VMEM)
    hbm = pl.BlockSpec(memory_space=pl.ANY)
    out = pl.pallas_call(
        body,
        out_shape=jax.ShapeDtypeStruct((CELLS, VARS * PATCH), BF16),
        in_specs=[vmem] * len(near) + [hbm] * len(far),
        out_specs=vmem,
        scratch_shapes=[
            pltpu.VMEM((GROUPS, COLS, 8, 128), BF16),
            pltpu.VMEM((GROUPS, COLS, 8, 128), BF16),
            pltpu.VMEM((CELLS, LEV * COLS * 8), BF16),
            pltpu.VMEM((4 * QUAD, CELLS), BF16),
            pltpu.VMEM((CELLS, 4 * QUAD), BF16),
            pltpu.VMEM((128, KDIM), BF16),
            pltpu.VMEM((GROUPS, SLOT, D), BF16),
            pltpu.VMEM((D, D), BF16),
            pltpu.VMEM((2, D, 3 * D), BF16),
            pltpu.VMEM((2, D, D), BF16),
            pltpu.VMEM((D, FF), BF16),
            pltpu.VMEM((FF, D), BF16),
            pltpu.VMEM((D, VARS * PATCH), BF16),
            pltpu.VMEM((KDIM, HEADS * 128), BF16),
            pltpu.VMEM((LEV * COLS * 8, KDIM), BF16),
            pltpu.VMEM((CELLS, D), BF16),
            pltpu.VMEM((16, QUAD, D), BF16),
            pltpu.VMEM((16 * QUAD, 2 * D), BF16),
            pltpu.VMEM((4 * QUAD, D), BF16),
            pltpu.SemaphoreType.DMA((GROUPS,)),
            pltpu.SemaphoreType.DMA((GROUPS,)),
            pltpu.SemaphoreType.DMA((12,)),
            pltpu.SemaphoreType.DMA((12,)),
            pltpu.SemaphoreType.DMA((12,)),
        ],
        compiler_params=pltpu.CompilerParams(
            collective_id=0, has_side_effects=True, vmem_limit_bytes=56 * 1024 * 1024
        ),
        name="forecast_step",
    )(*near, *far)
    return out.reshape(ROWS, COLS, LEV, VARS * PATCH).transpose(2, 0, 1, 3)


def solution(mesh):
    return jax.shard_map(
        per_device,
        mesh=mesh,
        in_specs=(P(("var", "lat"), None, None, "lon", None),) + (P(),) * 12,
        out_specs=P(None, ("var", "lat"), "lon", None),
        check_vma=False,
    )
```

time: 305 us -> 55.4 us (0.18); the launches traced: 301 us -> 55.1 us
  waiting for transfers between devices: 90.5 us -> 0 us
  local copies, waits for them, and re-layouts: 90.4 us -> 5.65 us
  other arithmetic: 64.6 us -> 0 us
  Pallas kernels: 0 us -> 49.5 us
  matrix products: 29.8 us -> 0 us
  starting transfers between devices: 25.5 us -> 0 us
    all_to_all x2 -> x0, waiting for transfers between devices: 83.7 us -> none  [the longest x1 63 us: sum_at_owner(): lax.all_to_all(tiles, axis, split_axis=0, concat_axis=0, tiled=True)]
    pallas_call x0 -> x1, Pallas kernels: none -> 49.5 us  [per_device(): pl.pallas_call(body, out_shape=jax.ShapeDtypeStruct((CELLS, VARS * PATCH)...]
    add x6 -> x0, other arithmetic: 45.1 us -> none  [the longest x3 33.7 us: add_var(): totals[0] + weights[..., None] * values]
    reshape x7 -> x2, local copies, waits for them, and re-layouts: 31.3 us -> 2.99 us  [the longest x1 1.71 us: per_device(): return out.reshape(ROWS, COLS, LEV, VARS * PATCH).transpose(2, 0, 1, 3)]
    dot_general x15 -> x0, matrix products: 28.2 us -> none  [the longest x3 8.88 us: add_var(): jnp.dot(patch.reshape(-1, patch_size), tab, preferred_element_type=jnp.fl...]
    all_to_all x2 -> x0, starting transfers between devices: 17.2 us -> none  [the longest x1 11.7 us: copy_for_each(): return lax.all_to_all(copies, axis, split_axis=0, concat_axis=0, tiled=True)]
    dynamic_slice x20 -> x0, local copies, waits for them, and re-layouts: 12.7 us -> none  [the longest x15 9.25 us: group_terms(): sums, _ = lax.scan(add_var, start, (patches, scores, table, offsets))]
    convert_element_type x4 -> x0, local copies, waits for them, and re-layouts: 11 us -> none  [the longest x1 7.8 us: per_device(): numerator.astype(jnp.bfloat16)]
  transfers between devices with their start and end apart: 6 -> 0, of which waited for: 4 -> 0; matrix products, arithmetic and copies ran while one was open for 4% -> 0% of each run, Pallas kernels for 0% -> 0%
where the time goes in v1:
time: 55.4 us; the launch traced here: 55.1 us
  Pallas kernels  49.5 us (89%)
  local copies, waits for them, and re-layouts  5.65 us (10%)
    pallas_call x1, Pallas kernels, per_device(): pl.pallas_call(body, out_shape=jax.ShapeDtypeStruct((CELLS, VARS * PATCH)...  49.5 us
    reshape x1, local copies, waits for them, and re-layouts, per_device(): return out.reshape(ROWS, COLS, LEV, VARS * PATCH).transpose(2, 0, 1, 3)  1.71 us
    reshape x1, local copies, waits for them, and re-layouts, per_device(): decode_bias.reshape(1, -1)  1.28 us
    pad x1, local copies, waits for them, and re-layouts, per_device(): offsets = jnp.pad(score_bias.T, ((0, 0), (0, 128 - VARS)))  1.28 us

profile of v1, /device:TPU:1, one launch (start us, length us, event | category | flops | bytes accessed | tf_op | source)
XLA Modules:
  0.0 55.1 jit_solution(7651649232600797415)
XLA Ops:
  0.0 1.3 %reshape.9.decode_bias_ref = f32[1,768]{1,0:T(1,128)} reshape(f32[768]{0:T(1024)} %param.33) | data formatting | bytes 6144 | tf_op jit(solution)/shard_map/reshape | solution.py:423
  1.3 1.3 %pad.9.score_bias_ref = f32[8,128]{1,0:T(8,128)} pad(f32[8,48]{1,0:T(8,128)} %bitcast.10, f32[]{:T(128)} %constant.20.clone.1), padding=0_0x0_80 | pad | bytes 5636 | tf_op jit(solution)/shard_map/jit(_pad)/pad | solution.py:415
  2.6 0.8 %copy.24 = bf16[48,16,8]{0,1,2:T(8,128)(2,1)S(1)} copy(bf16[48,16,8]{0,2,1:T(8,128)(2,1)} %param.22) | data formatting | bytes 24576 | tf_op args[1]
  3.3 0.6 %pad.8.score_tab_ref = bf16[8,16,128]{2,1,0:T(8,128)(2,1)} pad(bf16[8,16,48]{2,1,0:T(8,128)(2,1)S(1)} %bitcast.9, bf16[]{:T(256)} %constant.19.clone.1), padding=0_0x0_0x0_80 | pad | bytes 45058 | tf_op jit(solution)/shard_map/jit(_pad)/pad | solution.py:414
  3.9 49.5 %forecast_step.1 = bf16[144,768]{1,0:T(8,128)(2,1)} custom-call(bf16[3,2,12,16,96]{4,3,2,1,0:T(8,128)(2,1)} %bitcast.8, bf16[128,96]{1,0:T(8,128)(2,1)} %constant.21.clone.band_sel_ref, bf16[8,16,128]{2,1,0:T(8,128)(2,1)} %pad.8.score_tab_ref, f32[8,128]{1,0:T(8,128)} %pad.9.score_bias_ref, f32[48,512]{1,0:T(8,128)} %value_bias_ref.1, f32[4,512]{1,0:T(4,128)} %gains_ref.1, ...), custom_call_target="tpu_custom_call" | custom-call | tf_op jit(solution)/shard_map/forecast_step/pallas_call | solution.py:443
  53.4 1.7 %reshape.11 = bf16[6,12,2,768]{3,2,1,0:T(2,128)(2,1)} reshape(bf16[144,768]{1,0:T(8,128)(2,1)} %forecast_step.1) | data formatting | bytes 442368 | tf_op jit(solution)/shard_map/reshape | solution.py:479

commit v2 on v1

v2 whole, which is shorter than its diff:
```python
import functools

import jax
import jax.numpy as jnp
import numpy as np
from jax import lax
from jax.experimental import pallas as pl
from jax.experimental.pallas import tpu as pltpu
from jax.sharding import PartitionSpec as P

MESH = pl.DeviceIdType.MESH
EPSILON = 1e-05
F32 = jnp.float32
BF16 = jnp.bfloat16

GROUPS = 16
LONS = 16
LEV, ROWS, COLS = 2, 6, 12
CELLS = LEV * ROWS * COLS
LOCAL_VARS, PATCH, HEADS, HEAD_DIM = 3, 16, 8, 64
VARS = GROUPS * LOCAL_VARS
OWN = LOCAL_VARS * PATCH
D, FF = 512, 2048
PIECES = 18
WIDE = PIECES * OWN
SENT_LANES = 896
SLOT = 64
KDIM = GROUPS * SLOT
QUAD = 48
QUAD_CELLS = 36
SENT = 40


def cell_index(row, col, lev):
    return (row * COLS + col) * LEV + lev


def band_selector():
    out = np.zeros((GROUPS * 8, 4 * 128), np.float32)
    for band in range(GROUPS):
        for row in range(ROWS):
            out[band * 8 + row, band * ROWS + row] = 1
        for j in range(3):
            out[band * 8 + 6, 128 * (1 + j) + band * ROWS + j] = 1
            out[band * 8 + 7, 128 * (1 + j) + band * ROWS + 3 + j] = 1
    return out


def cell_selector():
    out = np.zeros((CELLS, CELLS), np.float32)
    for piece in range(PIECES):
        for k in range(8):
            if k < 6:
                pair, row = piece, k
            else:
                pair, row = PIECES + piece % 6, 3 * (k - 6) + piece // 6
            out[cell_index(row, pair % COLS, pair // COLS), piece * 8 + k] = 1
    return out


def quad_selector():
    out = np.zeros((4 * QUAD, CELLS), np.float32)
    for row in range(ROWS):
        for col in range(COLS):
            for lev in range(LEV):
                quad = (row // 3) * 2 + col // 6
                place = ((row % 3) * 6 + col % 6) * LEV + lev
                out[quad * QUAD + place, cell_index(row, col, lev)] = 1
    return out


def weight_spread():
    out = np.zeros((128, KDIM), np.float32)
    for group in range(GROUPS):
        for var in range(LOCAL_VARS):
            v, at = group * LOCAL_VARS + var, group * SLOT
            out[v, at + var * PATCH : at + (var + 1) * PATCH] = 1
            out[v, at + 48 + var] = 1
            out[v, at + 51 + var] = 1
    return out


def dot(a, b):
    return jnp.dot(a, b, preferred_element_type=F32)


def dot_t(a, b):
    return lax.dot_general(a, b, (((1,), (1,)), ((), ())), preferred_element_type=F32)


def iota(shape, dim):
    return lax.broadcasted_iota(jnp.int32, shape, dim)


def layer_norm(values, gain):
    shifted = values - jnp.mean(values, axis=-1, keepdims=True)
    spread = jnp.mean(shifted * shifted, axis=-1, keepdims=True)
    return shifted * lax.rsqrt(spread + EPSILON) * gain


def own_lanes(stacked, rows):
    head = iota((rows, 256), 1) // HEAD_DIM
    out = stacked[0:rows]
    for a in range(1, 4):
        out = jnp.where(head == a, stacked[a * rows : (a + 1) * rows], out)
    return out


def attention_four(q, k, v, allowed):
    rows = q.shape[0]
    head = iota((rows, 256), 1) // HEAD_DIM
    scaled = q * jnp.asarray(0.125, BF16)
    none = jnp.zeros_like(scaled)
    stacked = jnp.concatenate([jnp.where(head == a, scaled, none) for a in range(4)], axis=0)
    scores = dot_t(stacked, k)
    probs = []
    for a in range(4):
        part = scores[a * rows : (a + 1) * rows]
        if allowed is not None:
            part = jnp.where(allowed, part, -jnp.inf)
        raised = jnp.exp(part - jnp.max(part, axis=-1, keepdims=True))
        probs.append((raised * (1.0 / jnp.sum(raised, axis=-1, keepdims=True))).astype(BF16))
    return own_lanes(dot(jnp.concatenate(probs, axis=0), v), rows).astype(BF16)


def body(
    fields_hbm,
    band_sel_hbm,
    score_tab_hbm,
    score_bias_hbm,
    value_bias_hbm,
    value_tab_hbm,
    spread_hbm,
    cell_sel_hbm,
    agg_hbm,
    gains_hbm,
    qkv_hbm,
    proj_hbm,
    up_hbm,
    down_hbm,
    quad_sel_hbm,
    quad_back_hbm,
    decode_hbm,
    decode_bias_hbm,
    out_ref,
    fields,
    band_sel,
    score_tab,
    score_bias,
    value_bias,
    table,
    spread,
    cell_sel,
    agg,
    gains,
    qkv_w,
    proj_w,
    up_w,
    down_w,
    quad_sel,
    quad_back,
    decode_w,
    decode_bias,
    lifted,
    outgoing,
    incoming,
    score_wide,
    score_w,
    bias_wide,
    raw,
    weights_all,
    quads,
    window,
    context,
    returned,
    send_sem,
    recv_sem,
    halo_send,
    halo_recv,
    load_sem,
):
    var, lon, lat = lax.axis_index("var"), lax.axis_index("lon"), lax.axis_index("lat")
    band = var * 2 + lat
    up_band, down_band = lax.rem(band + GROUPS - 1, GROUPS), lax.rem(band + 1, GROUPS)
    left, right = lax.rem(lon + LONS - 1, LONS), lax.rem(lon + 1, LONS)

    def device(of_band, of_lon):
        return (of_band // 2, of_lon, lax.rem(of_band, 2))

    loads = {
        "fields": (fields_hbm, fields),
        "band_sel": (band_sel_hbm, band_sel),
        "score_tab": (score_tab_hbm, score_tab),
        "score_bias": (score_bias_hbm, score_bias),
        "value_bias": (value_bias_hbm, value_bias),
        "table": (value_tab_hbm, table.at[:, 0:OWN, :]),
        "spread": (spread_hbm, spread),
        "cell_sel": (cell_sel_hbm, cell_sel),
        "agg": (agg_hbm, agg),
        "gains": (gains_hbm, gains),
        "qkv0": (qkv_hbm.at[0], qkv_w.at[0]),
        "proj": (proj_hbm, proj_w),
        "up": (up_hbm, up_w),
        "down": (down_hbm, down_w),
        "quad_sel": (quad_sel_hbm, quad_sel),
        "qkv1": (qkv_hbm.at[1], qkv_w.at[1]),
        "quad_back": (quad_back_hbm, quad_back),
        "decode": (decode_hbm, decode_w),
        "decode_bias": (decode_bias_hbm, decode_bias),
    }
    loads = {
        name: pltpu.make_async_copy(a, b, load_sem.at[i]) for i, (name, (a, b)) in enumerate(loads.items())
    }
    loads["fields"].start()
    loads["band_sel"].start()

    barrier = pltpu.get_barrier_semaphore()
    peers = [device(lax.rem(band + k, GROUPS), lon) for k in range(1, GROUPS)]
    peers += [device(up_band, left), device(band, left), device(down_band, right), device(band, right)]
    for peer in peers:
        pl.semaphore_signal(barrier, inc=1, device_id=peer, device_id_type=MESH)

    lifted[...] = jnp.zeros(lifted.shape, BF16)
    loads["fields"].wait()
    loads["band_sel"].wait()
    rows = GROUPS * ROWS
    half = COLS // 2
    for v in range(LOCAL_VARS):
        lifted[0:COLS, v, :, 0:rows] = fields[v, 0]
        lifted[COLS:PIECES, v, :, 0:rows] = fields[v, 1, 0:half]
        for j in range(3):
            lifted[6 * j : 6 * j + 6, v, :, 128 * (1 + j) : 128 * (1 + j) + rows] = fields[v, 1, half:COLS]
    turned = dot_t(band_sel[...], lifted[...].reshape(WIDE, 512))
    outgoing[:, :, 0:WIDE] = turned.reshape(GROUPS, 8, WIDE).astype(BF16)

    pl.semaphore_wait(barrier, len(peers))

    sends = []
    for k in range(1, GROUPS):
        to = lax.rem(band + k, GROUPS)
        copy = pltpu.make_async_remote_copy(
            src_ref=outgoing.at[to],
            dst_ref=incoming.at[band],
            send_sem=send_sem.at[k],
            recv_sem=recv_sem.at[band],
            device_id=device(to, lon),
            device_id_type=MESH,
        )
        copy.start()
        sends.append(copy)
    own = pltpu.make_async_copy(outgoing.at[band], incoming.at[band], send_sem.at[0])
    own.start()
    for name, load in loads.items():
        if name not in ("fields", "band_sel"):
            load.start()

    shape = (GROUPS, 4, PATCH, 128)
    part = iota(shape, 1)
    match = (3 * iota(shape, 0) + part == iota(shape, 3)) & (part < 3)
    score_wide[...] = jnp.zeros(score_wide.shape, F32)
    bias_wide[...] = jnp.zeros(bias_wide.shape, F32)
    loads["score_tab"].wait()
    score_wide[:, :, 0:VARS] = score_tab[...].astype(F32)
    for h in range(HEADS):
        tab = jnp.broadcast_to(score_wide[:, h, :][None, None], shape)
        score_w[:, h * 128 : (h + 1) * 128] = jnp.where(match, tab, 0.0).reshape(KDIM, 128).astype(BF16)
    loads["score_bias"].wait()
    bias_wide[:, 0:VARS] = score_bias[...]
    loads["value_bias"].wait()
    bias = value_bias[...]
    bias_high = bias.astype(BF16)
    bias_low = (bias - bias_high.astype(F32)).astype(BF16)
    at_row, at_var = iota((GROUPS * 8, VARS), 0), iota((GROUPS * 8, VARS), 1)
    kind, first = at_row % 8, 3 * (at_row // 8)
    high = jnp.where((kind < 3) & (at_var == first + kind), 1.0, 0.0).astype(BF16)
    low = jnp.where((kind > 2) & (kind < 6) & (at_var == first + kind - 3), 1.0, 0.0).astype(BF16)
    bias_rows = dot(high, bias_high) + dot(low, bias_low)
    table[:, OWN : OWN + 8, :] = bias_rows.reshape(GROUPS, 8, D).astype(BF16)
    table[:, OWN + 8 : SLOT, :] = jnp.zeros((GROUPS, 8, D), BF16)
    window[:, SENT:QUAD, :] = jnp.zeros((4, QUAD - SENT, D), BF16)
    returned[:, SENT:QUAD, :] = jnp.zeros((4, QUAD - SENT, D), BF16)
    for name in ("table", "spread", "cell_sel"):
        loads[name].wait()

    own.wait()
    for k in range(1, GROUPS):
        source = lax.rem(band + GROUPS - k, GROUPS)
        pltpu.make_async_remote_copy(
            src_ref=outgoing.at[source],
            dst_ref=incoming.at[source],
            send_sem=send_sem.at[k],
            recv_sem=recv_sem.at[source],
            device_id=device(source, lon),
            device_id_type=MESH,
        ).wait_recv()

    lane = iota((8, 128), 1)
    in_first = lane < OWN
    in_second = (lane >= SLOT) & (lane < SLOT + OWN)
    ones = jnp.where((lane % SLOT >= OWN) & (lane % SLOT < OWN + 6), 1.0, 0.0)
    for j in range(GROUPS // 2):
        two = [incoming[2 * j].astype(F32), incoming[2 * j + 1].astype(F32)]
        for piece in range(PIECES):
            tile, at = divmod(piece * OWN, 128)
            moved = []
            for side in range(2):
                x = two[side][:, tile * 128 : (tile + 1) * 128]
                if at + OWN > 128:
                    x = jnp.where(lane >= at, x, two[side][:, (tile + 1) * 128 : (tile + 2) * 128])
                shift = (SLOT * side - at) % 128
                moved.append(pltpu.roll(x, shift, 1) if shift else x)
            raw[8 * piece : 8 * piece + 8, j * 128 : (j + 1) * 128] = jnp.where(
                in_first, moved[0], jnp.where(in_second, moved[1], ones)
            )
    cells = raw[...].astype(BF16)

    real = iota((CELLS, 128), 1) < VARS
    totals = []
    for h in range(HEADS):
        scores = dot(cells, score_w[:, h * 128 : (h + 1) * 128]) + bias_wide[h : h + 1, :]
        scores = jnp.where(real, scores, -jnp.inf)
        weights = jnp.exp(scores - jnp.max(scores, axis=-1, keepdims=True)).astype(BF16)
        totals.append(1.0 / jnp.sum(weights.astype(F32), axis=-1, keepdims=True))
        weights_all[h * CELLS : (h + 1) * CELLS, :] = weights
    all_table = table[...].reshape(KDIM, D)
    groups = []
    for g in range(2):
        own_weights = weights_all[4 * g * CELLS : 4 * (g + 1) * CELLS, :]
        sums = None
        for t in range(KDIM // 256):
            at = slice(t * 256, (t + 1) * 256)
            spread_w = dot(own_weights, spread[:, at]).astype(BF16)
            repeated = jnp.concatenate([cells[:, at]] * 4, axis=0)
            more = dot(repeated * spread_w, all_table[at, g * 256 : (g + 1) * 256])
            sums = more if sums is None else sums + more
        scaled = [sums[a * CELLS : (a + 1) * CELLS] * totals[4 * g + a] for a in range(4)]
        groups.append(own_lanes(jnp.concatenate(scaled, axis=0), CELLS).astype(BF16))
    pooled = jnp.concatenate(groups, axis=1)
    pooled = dot(cell_sel[...], pooled).astype(BF16)

    loads["agg"].wait()
    latent = dot(pooled, agg[...])

    loads["gains"].wait()
    normed = layer_norm(latent, gains[0:1, :]).astype(BF16)
    loads["qkv0"].wait()
    qkv = dot(normed, qkv_w[0]).astype(BF16)
    mixed = jnp.concatenate(
        [
            attention_four(
                qkv[:, at : at + 256], qkv[:, D + at : D + at + 256], qkv[:, 2 * D + at : 2 * D + at + 256], None
            )
            for at in (0, 256)
        ],
        axis=1,
    )
    loads["proj"].wait()
    hidden = latent + dot(mixed, proj_w[0])

    mixed = layer_norm(hidden, gains[1:2, :]).astype(BF16)
    loads["up"].wait()
    loads["down"].wait()
    latent = hidden
    for j in range(FF // D):
        at = slice(j * D, (j + 1) * D)
        active = jax.nn.gelu(dot(mixed, up_w[:, at]), approximate=True).astype(BF16)
        latent = latent + dot(active, down_w[at, :])

    normed = layer_norm(latent, gains[2:3, :]).astype(BF16)
    loads["quad_sel"].wait()
    quarters = dot(quad_sel[...], normed).astype(BF16).reshape(4, QUAD, D)
    quads[...] = quarters
    window[0] = quarters[3]
    owners = [device(up_band, left), device(up_band, lon), device(band, left)]
    users = [device(down_band, right), device(down_band, lon), device(band, right)]
    out_copies = []
    for quad in range(3):
        copy = pltpu.make_async_remote_copy(
            src_ref=quads.at[quad, 0:SENT],
            dst_ref=window.at[3 - quad, 0:SENT],
            send_sem=halo_send.at[quad],
            recv_sem=halo_recv.at[quad],
            device_id=owners[quad],
            device_id_type=MESH,
        )
        copy.start()
        out_copies.append(copy)

    at_query, at_key = iota((4 * QUAD, 4 * QUAD), 0), iota((4 * QUAD, 4 * QUAD), 1)
    allowed = (at_query % 2 == at_key % 2) & (at_key % QUAD < QUAD_CELLS)
    same_half = (at_query < 2 * QUAD) == (at_key < 2 * QUAD)
    allowed = allowed & (same_half | (band != GROUPS - 1))
    for name in ("qkv1", "quad_back", "decode", "decode_bias"):
        loads[name].wait()
    for copy in out_copies:
        copy.wait_recv()
    qkv = dot(window[...].reshape(4 * QUAD, D), qkv_w[1]).astype(BF16)
    for at in (0, 256):
        context[:, :, at : at + 256] = attention_four(
            qkv[:, at : at + 256], qkv[:, D + at : D + at + 256], qkv[:, 2 * D + at : 2 * D + at + 256], allowed
        ).reshape(4, QUAD, 256)
    returned[3] = context[0]
    back_copies = []
    for quad in range(3):
        copy = pltpu.make_async_remote_copy(
            src_ref=context.at[3 - quad, 0:SENT],
            dst_ref=returned.at[quad, 0:SENT],
            send_sem=halo_send.at[3 + quad],
            recv_sem=halo_recv.at[3 + quad],
            device_id=users[quad],
            device_id_type=MESH,
        )
        copy.start()
        back_copies.append(copy)
    for copy in back_copies:
        copy.wait_recv()
    mixed = dot(quad_back[...], returned[...].reshape(4 * QUAD, D)).astype(BF16)
    latent = latent + dot(mixed, proj_w[1])
    final = layer_norm(latent, gains[3:4, :]).astype(BF16)
    offsets = jnp.concatenate([decode_bias[i : i + 1, :] for i in range(VARS * PATCH // 128)], axis=1)
    out_ref[...] = (dot(final, decode_w[...]) + offsets).astype(BF16)

    for copy in sends + out_copies + back_copies:
        copy.wait_send()


def per_device(
    fields,
    score_table,
    score_bias,
    value_table,
    value_bias,
    agg_weight,
    qkv_weight,
    proj_weight,
    up_weight,
    down_weight,
    norm_gains,
    decode_weight,
    decode_bias,
):
    quads = quad_selector()
    operands = [
        fields.transpose(0, 1, 3, 4, 2),
        jnp.asarray(band_selector(), BF16),
        score_table.transpose(1, 2, 0),
        score_bias.T,
        value_bias,
        value_table.reshape(GROUPS, OWN, D),
        jnp.asarray(weight_spread(), BF16),
        jnp.asarray(cell_selector(), BF16),
        agg_weight,
        norm_gains,
        qkv_weight,
        proj_weight,
        up_weight,
        down_weight,
        jnp.asarray(quads, BF16),
        jnp.asarray(quads.T, BF16),
        decode_weight,
        decode_bias.reshape(-1, 128),
    ]
    own = [jax.ShapeDtypeStruct(x.shape, x.dtype) for x in operands]
    own[5] = jax.ShapeDtypeStruct((GROUPS, SLOT, D), BF16)
    out = pl.pallas_call(
        body,
        out_shape=jax.ShapeDtypeStruct((CELLS, VARS * PATCH), BF16),
        in_specs=[pl.BlockSpec(memory_space=pl.ANY)] * len(operands),
        out_specs=pl.BlockSpec(memory_space=pltpu.VMEM),
        scratch_shapes=[pltpu.VMEM(x.shape, x.dtype) for x in own]
        + [
            pltpu.VMEM((PIECES, LOCAL_VARS, PATCH, 512), BF16),
            pltpu.VMEM((GROUPS, 8, SENT_LANES), BF16),
            pltpu.VMEM((GROUPS, 8, SENT_LANES), BF16),
            pltpu.VMEM((PATCH, HEADS, 128), F32),
            pltpu.VMEM((KDIM, HEADS * 128), BF16),
            pltpu.VMEM((HEADS, 128), F32),
            pltpu.VMEM((CELLS, KDIM), F32),
            pltpu.VMEM((HEADS * CELLS, 128), BF16),
            pltpu.VMEM((4, QUAD, D), BF16),
            pltpu.VMEM((4, QUAD, D), BF16),
            pltpu.VMEM((4, QUAD, D), BF16),
            pltpu.VMEM((4, QUAD, D), BF16),
            pltpu.SemaphoreType.DMA((GROUPS,)),
            pltpu.SemaphoreType.DMA((GROUPS,)),
            pltpu.SemaphoreType.DMA((6,)),
            pltpu.SemaphoreType.DMA((6,)),
            pltpu.SemaphoreType.DMA((len(operands) + 1,)),
        ],
        compiler_params=pltpu.CompilerParams(
            collective_id=0, has_side_effects=True, vmem_limit_bytes=56 * 1024 * 1024
        ),
        name="forecast_step",
    )(*operands)
    return out.reshape(ROWS, COLS, LEV, VARS * PATCH).transpose(2, 0, 1, 3)


def solution(mesh):
    return jax.shard_map(
        per_device,
        mesh=mesh,
        in_specs=(P(("var", "lat"), None, None, "lon", None),) + (P(),) * 12,
        out_specs=P(None, ("var", "lat"), "lon", None),
        check_vma=False,
    )
```

time: 55.4 us -> 39.8 us (0.72)
  Pallas kernels: 49.5 us -> 38 us
  local copies, waits for them, and re-layouts: 5.65 us -> 1.71 us
    pallas_call x1, Pallas kernels: 49.5 us -> 38 us  [per_device(): pl.pallas_call(body, out_shape=jax.ShapeDtypeStruct((CELLS, VARS * PATCH)...]
    pad x2 -> x0, local copies, waits for them, and re-layouts: 1.9 us -> none  [the longest x1 1.28 us: per_device(): offsets = jnp.pad(score_bias.T, ((0, 0), (0, 128 - VARS)))]
    reshape x1 -> x0, local copies, waits for them, and re-layouts: 1.28 us -> none  [per_device(): decode_bias.reshape(1, -1)]
    unnamed x1 -> x0, local copies, waits for them, and re-layouts: 0.76 us -> none
where the time goes in v2:
time: 39.8 us; the launch traced here: 39.7 us
  Pallas kernels  38 us (95%)
  local copies, waits for them, and re-layouts  1.71 us (4%)
    pallas_call x1, Pallas kernels, per_device(): pl.pallas_call(body, out_shape=jax.ShapeDtypeStruct((CELLS, VARS * PATCH)...  38 us
    reshape x1, local copies, waits for them, and re-layouts, per_device(): return out.reshape(ROWS, COLS, LEV, VARS * PATCH).transpose(2, 0, 1, 3)  1.71 us

profile of v2, /device:TPU:1, one launch (start us, length us, event | category | flops | bytes accessed | tf_op | source)
XLA Modules:
  0.0 39.7 jit_solution(7799183087547396550)
XLA Ops:
  0.0 38.0 %forecast_step.1 = bf16[144,768]{1,0:T(8,128)(2,1)} custom-call(bf16[3,2,12,16,96]{4,3,2,1,0:T(8,128)(2,1)} %bitcast.7, bf16[128,512]{1,0:T(8,128)(2,1)} %constant.10.clone.band_sel_hbm, bf16[16,8,48]{2,1,0:T(8,128)(2,1)} %bitcast.8, f32[8,48]{1,0:T(8,128)} %bitcast.9, f32[48,512]{1,0:T(8,128)} %value_bias_hbm.1, bf16[16,48,512]{2,1,0:T(8,128)(2,1)} %bitcast.6, ...), custom_call_target="tpu_custom_call" | custom-call | tf_op jit(solution)/shard_map/forecast_step/pallas_call | solution.py:465
  38.0 1.7 %reshape.11 = bf16[6,12,2,768]{3,2,1,0:T(2,128)(2,1)} reshape(bf16[144,768]{1,0:T(8,128)(2,1)} %forecast_step.1) | data formatting | bytes 442368 | tf_op jit(solution)/shard_map/reshape | solution.py:495

commit v3 on v2

--- a/solution.py
+++ b/solution.py
@@ -173,6 +173,8 @@
     window,
     context,
     returned,
+    edge,
+    edge_context,
     send_sem,
     recv_sem,
     halo_send,
@@ -279,26 +281,32 @@
     table[:, OWN + 8 : SLOT, :] = jnp.zeros((GROUPS, 8, D), BF16)
     window[:, SENT:QUAD, :] = jnp.zeros((4, QUAD - SENT, D), BF16)
     returned[:, SENT:QUAD, :] = jnp.zeros((4, QUAD - SENT, D), BF16)
+    edge[:, SENT:QUAD, :] = jnp.zeros((2, QUAD - SENT, D), BF16)
+    first_band, last_band = band == 0, band == GROUPS - 1
+
+    @pl.when(first_band)
+    def _():
+        window[2:4, 0:SENT, :] = jnp.zeros((2, SENT, D), BF16)
+
     for name in ("table", "spread", "cell_sel"):
         loads[name].wait()
 
     own.wait()
-    for k in range(1, GROUPS):
-        source = lax.rem(band + GROUPS - k, GROUPS)
-        pltpu.make_async_remote_copy(
-            src_ref=outgoing.at[source],
-            dst_ref=incoming.at[source],
-            send_sem=send_sem.at[k],
-            recv_sem=recv_sem.at[source],
-            device_id=device(source, lon),
-            device_id_type=MESH,
-        ).wait_recv()
-
     lane = iota((8, 128), 1)
     in_first = lane < OWN
     in_second = (lane >= SLOT) & (lane < SLOT + OWN)
     ones = jnp.where((lane % SLOT >= OWN) & (lane % SLOT < OWN + 6), 1.0, 0.0)
     for j in range(GROUPS // 2):
+        for source in (2 * j, 2 * j + 1):
+            arrival = pltpu.make_async_remote_copy(
+                src_ref=outgoing.at[source],
+                dst_ref=incoming.at[source],
+                send_sem=send_sem.at[source],
+                recv_sem=recv_sem.at[source],
+                device_id=device(source, lon),
+                device_id_type=MESH,
+            )
+            pl.when(band != source)(arrival.wait_recv)
         two = [incoming[2 * j].astype(F32), incoming[2 * j + 1].astype(F32)]
         for piece in range(PIECES):
             tile, at = divmod(piece * OWN, 128)
@@ -370,58 +378,109 @@
     loads["quad_sel"].wait()
     quarters = dot(quad_sel[...], normed).astype(BF16).reshape(4, QUAD, D)
     quads[...] = quarters
-    window[0] = quarters[3]
-    owners = [device(up_band, left), device(up_band, lon), device(band, left)]
-    users = [device(down_band, right), device(down_band, lon), device(band, right)]
-    out_copies = []
-    for quad in range(3):
-        copy = pltpu.make_async_remote_copy(
-            src_ref=quads.at[quad, 0:SENT],
-            dst_ref=window.at[3 - quad, 0:SENT],
-            send_sem=halo_send.at[quad],
-            recv_sem=halo_recv.at[quad],
-            device_id=owners[quad],
+    window[0] = quarters[0]
+
+    def halo(source, target, sent, arrived, to):
+        return pltpu.make_async_remote_copy(
+            src_ref=source,
+            dst_ref=target,
+            send_sem=halo_send.at[sent],
+            recv_sem=halo_recv.at[arrived],
+            device_id=to,
             device_id_type=MESH,
         )
-        copy.start()
-        out_copies.append(copy)
+
+    rows = slice(0, SENT)
+    out_right = halo(quads.at[1, rows], window.at[1, rows], 0, 0, device(band, right))
+    out_down = halo(quads.at[2, rows], window.at[2, rows], 1, 1, device(down_band, lon))
+    out_corner = halo(quads.at[3, rows], window.at[3, rows], 2, 2, device(down_band, right))
+    out_edge = halo(quads.at[3, rows], edge.at[1, rows], 3, 3, device(band, right))
+    back_left = halo(context.at[1, rows], returned.at[1, rows], 4, 4, device(band, left))
+    back_up = halo(context.at[2, rows], returned.at[2, rows], 5, 5, device(up_band, lon))
+    back_corner = halo(context.at[3, rows], returned.at[3, rows], 6, 6, device(up_band, left))
+    back_edge = halo(edge_context.at[1, rows], returned.at[3, rows], 7, 6, device(band, left))
+
+    @pl.when(jnp.logical_not(last_band))
+    def _():
+        out_corner.start()
+        out_down.start()
+
+    out_right.start()
+
+    @pl.when(last_band)
+    def _():
+        out_edge.start()
+        edge[0] = quads[2]
 
     at_query, at_key = iota((4 * QUAD, 4 * QUAD), 0), iota((4 * QUAD, 4 * QUAD), 1)
-    allowed = (at_query % 2 == at_key % 2) & (at_key % QUAD < QUAD_CELLS)
+    same_level = (at_query % 2 == at_key % 2) & (at_key % QUAD < QUAD_CELLS)
     same_half = (at_query < 2 * QUAD) == (at_key < 2 * QUAD)
-    allowed = allowed & (same_half | (band != GROUPS - 1))
+    allowed = same_level & (same_half | jnp.logical_not(first_band))
     for name in ("qkv1", "quad_back", "decode", "decode_bias"):
         loads[name].wait()
-    for copy in out_copies:
-        copy.wait_recv()
-    qkv = dot(window[...].reshape(4 * QUAD, D), qkv_w[1]).astype(BF16)
-    for at in (0, 256):
-        context[:, :, at : at + 256] = attention_four(
-            qkv[:, at : at + 256], qkv[:, D + at : D + at + 256], qkv[:, 2 * D + at : 2 * D + at + 256], allowed
-        ).reshape(4, QUAD, 256)
-    returned[3] = context[0]
-    back_copies = []
-    for quad in range(3):
-        copy = pltpu.make_async_remote_copy(
-            src_ref=context.at[3 - quad, 0:SENT],
-            dst_ref=returned.at[quad, 0:SENT],
-            send_sem=halo_send.at[3 + quad],
-            recv_sem=halo_recv.at[3 + quad],
-            device_id=users[quad],
-            device_id_type=MESH,
-        )
-        copy.start()
-        back_copies.append(copy)
-    for copy in back_copies:
-        copy.wait_recv()
+
+    def window_context(cells_in, out, mask):
+        count = 4 if out is context else 2
+        qkv = dot(cells_in[...].reshape(count * QUAD, D), qkv_w[1]).astype(BF16)
+        for at in (0, 256):
+            out[:, :, at : at + 256] = attention_four(
+                qkv[:, at : at + 256], qkv[:, D + at : D + at + 256], qkv[:, 2 * D + at : 2 * D + at + 256], mask
+            ).reshape(count, QUAD, 256)
+
+    out_right.wait_recv()
+
+    @pl.when(jnp.logical_not(first_band))
+    def _():
+        out_down.wait_recv()
+        out_corner.wait_recv()
+
+    window_context(window, context, allowed)
+
+    @pl.when(jnp.logical_not(first_band))
+    def _():
+        back_corner.start()
+        back_up.start()
+
+    back_left.start()
+    returned[0] = context[0]
+
+    @pl.when(last_band)
+    def _():
+        out_edge.wait_recv()
+        window_context(edge, edge_context, same_level[0 : 2 * QUAD, 0 : 2 * QUAD])
+        back_edge.start()
+        returned[2] = edge_context[0]
+
+    back_left.wait_recv()
+    back_corner.wait_recv()
+
+    @pl.when(jnp.logical_not(last_band))
+    def _():
+        back_up.wait_recv()
+
     mixed = dot(quad_back[...], returned[...].reshape(4 * QUAD, D)).astype(BF16)
     latent = latent + dot(mixed, proj_w[1])
     final = layer_norm(latent, gains[3:4, :]).astype(BF16)
     offsets = jnp.concatenate([decode_bias[i : i + 1, :] for i in range(VARS * PATCH // 128)], axis=1)
-    out_ref[...] = (dot(final, decode_w[...]) + offsets).astype(BF16)
-
-    for copy in sends + out_copies + back_copies:
+    out_ref[...] = (dot(final, decode_w[...]) + offsets).astype(BF16).reshape(CELLS // LEV, LEV, VARS * PATCH)
+
+    for copy in sends + [out_right, back_left]:
         copy.wait_send()
+
+    @pl.when(jnp.logical_not(last_band))
+    def _():
+        out_down.wait_send()
+        out_corner.wait_send()
+
+    @pl.when(jnp.logical_not(first_band))
+    def _():
+        back_up.wait_send()
+        back_corner.wait_send()
+
+    @pl.when(last_band)
+    def _():
+        out_edge.wait_send()
+        back_edge.wait_send()
 
 
 def per_device(
@@ -464,7 +523,7 @@
     own[5] = jax.ShapeDtypeStruct((GROUPS, SLOT, D), BF16)
     out = pl.pallas_call(
         body,
-        out_shape=jax.ShapeDtypeStruct((CELLS, VARS * PATCH), BF16),
+        out_shape=jax.ShapeDtypeStruct((CELLS // LEV, LEV, VARS * PATCH), BF16),
         in_specs=[pl.BlockSpec(memory_space=pl.ANY)] * len(operands),
         out_specs=pl.BlockSpec(memory_space=pltpu.VMEM),
         scratch_shapes=[pltpu.VMEM(x.shape, x.dtype) for x in own]
@@ -481,10 +540,12 @@
             pltpu.VMEM((4, QUAD, D), BF16),
             pltpu.VMEM((4, QUAD, D), BF16),
             pltpu.VMEM((4, QUAD, D), BF16),
+            pltpu.VMEM((2, QUAD, D), BF16),
+            pltpu.VMEM((2, QUAD, D), BF16),
             pltpu.SemaphoreType.DMA((GROUPS,)),
             pltpu.SemaphoreType.DMA((GROUPS,)),
-            pltpu.SemaphoreType.DMA((6,)),
-            pltpu.SemaphoreType.DMA((6,)),
+            pltpu.SemaphoreType.DMA((8,)),
+            pltpu.SemaphoreType.DMA((8,)),
             pltpu.SemaphoreType.DMA((len(operands) + 1,)),
         ],
         compiler_params=pltpu.CompilerParams(

time: 39.8 us -> 38.4 us (0.965); the launches traced: 39.7 us -> 37.8 us
  Pallas kernels: 38 us -> 36 us
    pallas_call x1, Pallas kernels: 38 us -> 36 us  [per_device(): pl.pallas_call(body, out_shape=jax.ShapeDtypeStruct((CELLS // LEV, LEV, V...]
    unnamed x0 -> x1, local copies, waits for them, and re-layouts: none -> 1.77 us
    reshape x1 -> x0, local copies, waits for them, and re-layouts: 1.71 us -> none  [per_device(): return out.reshape(ROWS, COLS, LEV, VARS * PATCH).transpose(2, 0, 1, 3)]
where the time goes in v3:
time: 38.4 us; the launch traced here: 37.8 us
  Pallas kernels  36 us (94%)
  local copies, waits for them, and re-layouts  1.77 us (5%)
    pallas_call x1, Pallas kernels, per_device(): pl.pallas_call(body, out_shape=jax.ShapeDtypeStruct((CELLS // LEV, LEV, V...  36 us
    unnamed x1, local copies, waits for them, and re-layouts  1.77 us

profile of v3, /device:TPU:1, one launch (start us, length us, event | category | flops | bytes accessed | tf_op | source)
XLA Modules:
  0.0 37.8 jit_solution(4743039510571890349)
XLA Ops:
  0.0 36.0 %forecast_step.1 = bf16[72,2,768]{2,1,0:T(2,128)(2,1)} custom-call(bf16[3,2,12,16,96]{4,3,2,1,0:T(8,128)(2,1)} %bitcast.10, bf16[128,512]{1,0:T(8,128)(2,1)} %constant.10.clone.band_sel_hbm, bf16[16,8,48]{2,1,0:T(8,128)(2,1)} %bitcast.11, f32[8,48]{1,0:T(8,128)} %bitcast.12, f32[48,512]{1,0:T(8,128)} %value_bias_hbm.1, bf16[16,48,512]{2,1,0:T(8,128)(2,1)} %bitcast.9, ...), custom_call_target="tpu_custom_call" | custom-call | tf_op jit(solution)/shard_map/forecast_step/pallas_call | solution.py:524
  36.0 1.8 %copy.20 = bf16[2,6,12,768]{3,0,2,1:T(2,128)(2,1)} copy(bf16[2,6,12,768]{3,0,2,1:T(2,128)(2,1)} %bitcast.8) | data formatting | bytes 442368

commit v4 on v3

--- a/solution.py
+++ b/solution.py
@@ -17,6 +17,7 @@
 LONS = 16
 LEV, ROWS, COLS = 2, 6, 12
 CELLS = LEV * ROWS * COLS
+HALF = CELLS // 2
 LOCAL_VARS, PATCH, HEADS, HEAD_DIM = 3, 16, 8, 64
 VARS = GROUPS * LOCAL_VARS
 OWN = LOCAL_VARS * PATCH
@@ -239,7 +240,7 @@
 
     sends = []
     for k in range(1, GROUPS):
-        to = lax.rem(band + k, GROUPS)
+        to = k - 1 + (k - 1 >= band).astype(jnp.int32)
         copy = pltpu.make_async_remote_copy(
             src_ref=outgoing.at[to],
             dst_ref=incoming.at[band],
@@ -325,7 +326,9 @@
     real = iota((CELLS, 128), 1) < VARS
     totals = []
     for h in range(HEADS):
-        scores = dot(cells, score_w[:, h * 128 : (h + 1) * 128]) + bias_wide[h : h + 1, :]
+        if h % 2 == 0:
+            both = dot(cells, score_w[:, h * 128 : (h + 2) * 128])
+        scores = both[:, h % 2 * 128 : (h % 2 + 1) * 128] + bias_wide[h : h + 1, :]
         scores = jnp.where(real, scores, -jnp.inf)
         weights = jnp.exp(scores - jnp.max(scores, axis=-1, keepdims=True)).astype(BF16)
         totals.append(1.0 / jnp.sum(weights.astype(F32), axis=-1, keepdims=True))
@@ -365,20 +368,9 @@
     loads["proj"].wait()
     hidden = latent + dot(mixed, proj_w[0])
 
-    mixed = layer_norm(hidden, gains[1:2, :]).astype(BF16)
     loads["up"].wait()
     loads["down"].wait()
-    latent = hidden
-    for j in range(FF // D):
-        at = slice(j * D, (j + 1) * D)
-        active = jax.nn.gelu(dot(mixed, up_w[:, at]), approximate=True).astype(BF16)
-        latent = latent + dot(active, down_w[at, :])
-
-    normed = layer_norm(latent, gains[2:3, :]).astype(BF16)
     loads["quad_sel"].wait()
-    quarters = dot(quad_sel[...], normed).astype(BF16).reshape(4, QUAD, D)
-    quads[...] = quarters
-    window[0] = quarters[0]
 
     def halo(source, target, sent, arrived, to):
         return pltpu.make_async_remote_copy(
@@ -400,18 +392,32 @@
     back_corner = halo(context.at[3, rows], returned.at[3, rows], 6, 6, device(up_band, left))
     back_edge = halo(edge_context.at[1, rows], returned.at[3, rows], 7, 6, device(band, left))
 
-    @pl.when(jnp.logical_not(last_band))
-    def _():
-        out_corner.start()
-        out_down.start()
+    ended = [None, None]
+    for lower in (1, 0):
+        latent = hidden[lower * HALF : (lower + 1) * HALF]
+        mixed = layer_norm(latent, gains[1:2, :]).astype(BF16)
+        for j in range(FF // D):
+            at = slice(j * D, (j + 1) * D)
+            active = jax.nn.gelu(dot(mixed, up_w[:, at]), approximate=True).astype(BF16)
+            latent = latent + dot(active, down_w[at, :])
+        ended[lower] = latent
+        normed = layer_norm(latent, gains[2:3, :]).astype(BF16)
+        quads[2 * lower : 2 * lower + 2] = dot(quad_sel[...], normed).astype(BF16).reshape(2, QUAD, D)
+        if lower:
+
+            @pl.when(jnp.logical_not(last_band))
+            def _():
+                out_corner.start()
+                out_down.start()
+
+            @pl.when(last_band)
+            def _():
+                out_edge.start()
+                edge[0] = quads[2]
 
     out_right.start()
-
-    @pl.when(last_band)
-    def _():
-        out_edge.start()
-        edge[0] = quads[2]
-
+    window[0] = quads[0]
+    latent = jnp.concatenate(ended, axis=0)
     at_query, at_key = iota((4 * QUAD, 4 * QUAD), 0), iota((4 * QUAD, 4 * QUAD), 1)
     same_level = (at_query % 2 == at_key % 2) & (at_key % QUAD < QUAD_CELLS)
     same_half = (at_query < 2 * QUAD) == (at_key < 2 * QUAD)
@@ -514,7 +520,7 @@
         proj_weight,
         up_weight,
         down_weight,
-        jnp.asarray(quads, BF16),
+        jnp.asarray(quads[0 : 2 * QUAD, 0:HALF], BF16),
         jnp.asarray(quads.T, BF16),
         decode_weight,
         decode_bias.reshape(-1, 128),
@@ -523,7 +529,7 @@
     own[5] = jax.ShapeDtypeStruct((GROUPS, SLOT, D), BF16)
     out = pl.pallas_call(
         body,
-        out_shape=jax.ShapeDtypeStruct((CELLS // LEV, LEV, VARS * PATCH), BF16),
+        out_shape=pltpu.VMEM((CELLS // LEV, LEV, VARS * PATCH), BF16),
         in_specs=[pl.BlockSpec(memory_space=pl.ANY)] * len(operands),
         out_specs=pl.BlockSpec(memory_space=pltpu.VMEM),
         scratch_shapes=[pltpu.VMEM(x.shape, x.dtype) for x in own]

time: 38.4 us -> 34.9 us (0.909)
  the two profiles are of different devices: /device:TPU:1 before, /device:TPU:64 now
where the time goes in v4:
time: 34.9 us; the launch traced here: 34.8 us
  Pallas kernels  34.1 us (98%)
  local copies, waits for them, and re-layouts  0.69 us (2%)
    pallas_call x1, Pallas kernels, per_device(): pl.pallas_call(body, out_shape=pltpu.VMEM((CELLS // LEV, LEV, VARS * PATC...  34.1 us

profile of v4, /device:TPU:64, one launch (start us, length us, event | category | flops | bytes accessed | tf_op | source)
XLA Modules:
  0.0 34.8 jit_solution(7581869185989528486)
XLA Ops:
  0.0 34.1 %forecast_step.1 = bf16[72,2,768]{2,1,0:T(2,128)(2,1)S(1)} custom-call(bf16[3,2,12,16,96]{4,3,2,1,0:T(8,128)(2,1)} %bitcast.10, bf16[128,512]{1,0:T(8,128)(2,1)} %constant.10.clone.band_sel_hbm, bf16[16,8,48]{2,1,0:T(8,128)(2,1)} %bitcast.11, f32[8,48]{1,0:T(8,128)} %bitcast.12, f32[48,512]{1,0:T(8,128)} %value_bias_hbm.1, bf16[16,48,512]{2,1,0:T(8,128)(2,1)} %bitcast.9, ...), custom_call_target="tpu_custom_call" | custom-call | tf_op jit(solution)/shard_map/forecast_step/pallas_call | solution.py:530
  34.1 0.7 %copy.20 = bf16[2,6,12,768]{3,0,2,1:T(2,128)(2,1)} copy(bf16[2,6,12,768]{3,0,2,1:T(2,128)(2,1)S(1)} %bitcast.8) | data formatting | bytes 442368

commit v5 on v4

--- a/solution.py
+++ b/solution.py
@@ -233,13 +233,19 @@
         lifted[COLS:PIECES, v, :, 0:rows] = fields[v, 1, 0:half]
         for j in range(3):
             lifted[6 * j : 6 * j + 6, v, :, 128 * (1 + j) : 128 * (1 + j) + rows] = fields[v, 1, half:COLS]
-    turned = dot_t(band_sel[...], lifted[...].reshape(WIDE, 512))
-    outgoing[:, :, 0:WIDE] = turned.reshape(GROUPS, 8, WIDE).astype(BF16)
+
+    def turn(first, count):
+        turned = dot_t(band_sel[first * 8 : (first + count) * 8, :], lifted[...].reshape(WIDE, 512))
+        outgoing[first : first + count, :, 0:WIDE] = turned.reshape(count, 8, WIDE).astype(BF16)
+
+    turn(0, GROUPS // 2)
 
     pl.semaphore_wait(barrier, len(peers))
 
     sends = []
     for k in range(1, GROUPS):
+        if k == GROUPS // 2:
+            turn(GROUPS // 2, GROUPS // 2)
         to = k - 1 + (k - 1 >= band).astype(jnp.int32)
         copy = pltpu.make_async_remote_copy(
             src_ref=outgoing.at[to],

time: 34.9 us -> 34.9 us (level)
  no operation moved by 1% of the time
where the time goes in v5:
time: 34.9 us; the launch traced here: 34.8 us
  Pallas kernels  34.2 us (98%)
  local copies, waits for them, and re-layouts  0.69 us (2%)
    pallas_call x1, Pallas kernels, per_device(): pl.pallas_call(body, out_shape=pltpu.VMEM((CELLS // LEV, LEV, VARS * PATC...  34.2 us

profile of v5, /device:TPU:64, one launch (start us, length us, event | category | flops | bytes accessed | tf_op | source)
XLA Modules:
  0.0 34.8 jit_solution(2971627625424931518)
XLA Ops:
  0.0 34.2 %forecast_step.1 = bf16[72,2,768]{2,1,0:T(2,128)(2,1)S(1)} custom-call(bf16[3,2,12,16,96]{4,3,2,1,0:T(8,128)(2,1)} %bitcast.10, bf16[128,512]{1,0:T(8,128)(2,1)} %constant.10.clone.band_sel_hbm, bf16[16,8,48]{2,1,0:T(8,128)(2,1)} %bitcast.11, f32[8,48]{1,0:T(8,128)} %bitcast.12, f32[48,512]{1,0:T(8,128)} %value_bias_hbm.1, bf16[16,48,512]{2,1,0:T(8,128)(2,1)} %bitcast.9, ...), custom_call_target="tpu_custom_call" | custom-call | tf_op jit(solution)/shard_map/forecast_step/pallas_call | solution.py:536
  34.2 0.7 %copy.20 = bf16[2,6,12,768]{3,0,2,1:T(2,128)(2,1)} copy(bf16[2,6,12,768]{3,0,2,1:T(2,128)(2,1)S(1)} %bitcast.8) | data formatting | bytes 442368
